TPU v7x, 128 devices: a whole 4x4x4 slice. The times are simulated.
128 devices in a mesh: section: 4 (over y_lo, core), dp: 32 (over z, x, y_hi).
Axes of the slice: x: 4, y: 4 (y_hi: 2, y_lo: 2; y = y_hi * 2 + y_lo), z: 4, core: 2. Of those that a mesh axis runs over, the one named last changes fastest.
Arguments:
- inputs: bfloat16 [4, 4096, 2048], P(None, 'dp'), may hold values from -6 to 6
- cotangent: bfloat16 [4, 4096, 2048], P(None, 'dp'), may hold values from -0.046875 to 0.046875
- weights: bfloat16 [4, 2048, 2048], P('section'), may hold values from -0.125 to 0.125
- preconds: float32 [4, 32, 64, 64], P('section', 'dp'), may hold values from -0.75 to 0.75
- order: int32 [32, 4], P('dp'), may hold values from 0 to 3, each once within a row
- owner: int32 [32], replicated, may hold values from 0 to 31, each once
Outputs:
- precond: bfloat16 [4, 2048, 2048], P('section')
- gram: float32 [4, 32, 64, 64], P('section', 'dp')
Inputs may be any that keep to these rules, and one draw needn't show every extreme that they name: `order`: for each index of dp, each plan slot runs a different micro-batch. `owner`: each device of dp owns exactly one block.
All inputs are finite; a program needn't handle non-finite values.
Results may differ from a plain program's by a relative error of at most 0.013.
Values may be sent and summed in bfloat16 or wider, within the bound.
A program may use at most 128 MiB of HBM per device.

v0:
```python
import jax
import jax.numpy as jnp
from jax import lax
from jax.sharding import PartitionSpec as P

coef = 0.7978845608028654
cubic = 0.044715


def passed_along(block, axis, distance):
    devices = range(lax.axis_size(axis))
    route = [(i - distance, i) for i in devices if i - distance in devices]
    return lax.ppermute(block, axis, route)


def gelu_value(z):
    tanh_part = jnp.tanh(coef * (z + cubic * z * z * z))
    return 0.5 * z * (1.0 + tanh_part)


def gelu_slope(z):
    tanh_part = jnp.tanh(coef * (z + cubic * z * z * z))
    return 0.5 * (1.0 + tanh_part) + 0.5 * z * (1.0 - tanh_part * tanh_part) * coef * (
        1.0 + 3.0 * cubic * z * z
    )


def body(inputs, cotangent, weights, preconds, order, owner):
    weight = weights[0]
    sections = lax.axis_size("section")
    place = lax.axis_index("section")
    n_micro = inputs.shape[0]
    tok_rows = inputs.shape[1]
    width = inputs.shape[2]
    n_group = owner.shape[0]
    block = width // n_group
    total_rows = n_micro * tok_rows * n_group
    n_steps = n_micro + sections - 1
    feed = jnp.take(inputs, order[0], axis=0)
    saved_in = jnp.zeros((n_micro, tok_rows, width), jnp.bfloat16)
    saved_pre = jnp.zeros((n_micro, tok_rows, width), jnp.float32)

    def forward_step(carry, step):
        incoming, kept_in, kept_pre = carry
        slot = step - place
        valid = (slot >= 0) & (slot < n_micro)
        slot_c = jnp.clip(slot, 0, n_micro - 1)
        first = lax.dynamic_index_in_dim(feed, slot_c, 0, keepdims=False)
        current = jnp.where(place == 0, first, incoming)
        pre = jnp.dot(current, weight, preferred_element_type=jnp.float32)
        output = (current.astype(jnp.float32) + gelu_value(pre)).astype(jnp.bfloat16)
        old_in = lax.dynamic_index_in_dim(kept_in, slot_c, 0, keepdims=False)
        kept_in = lax.dynamic_update_index_in_dim(
            kept_in, jnp.where(valid, current, old_in), slot_c, 0
        )
        old_pre = lax.dynamic_index_in_dim(kept_pre, slot_c, 0, keepdims=False)
        kept_pre = lax.dynamic_update_index_in_dim(
            kept_pre, jnp.where(valid, pre, old_pre), slot_c, 0
        )
        incoming = passed_along(output, "section", 1)
        return ((incoming, kept_in, kept_pre), None)

    start_rows = jnp.zeros((tok_rows, width), jnp.bfloat16)
    (unused_rows, saved_in, saved_pre), _ = lax.scan(
        forward_step, (start_rows, saved_in, saved_pre), jnp.arange(n_steps, dtype=jnp.int32)
    )

    def backward_step(carry, step):
        incoming, grad_sum = carry
        slot = step - (sections - 1 - place)
        valid = (slot >= 0) & (slot < n_micro)
        slot_c = jnp.clip(slot, 0, n_micro - 1)
        last = lax.dynamic_index_in_dim(cotangent, slot_c, 0, keepdims=False)
        current = jnp.where(place == sections - 1, last, incoming)
        current = jnp.where(valid, current, jnp.zeros_like(current))
        acts = lax.dynamic_index_in_dim(saved_in, slot_c, 0, keepdims=False)
        pre = lax.dynamic_index_in_dim(saved_pre, slot_c, 0, keepdims=False)
        slopes = (current.astype(jnp.float32) * gelu_slope(pre)).astype(jnp.bfloat16)
        grad_sum = grad_sum + lax.dot_general(
            acts, slopes, (((0,), (0,)), ((), ())), preferred_element_type=jnp.float32
        )
        back = lax.dot_general(
            slopes, weight, (((1,), (1,)), ((), ())), preferred_element_type=jnp.float32
        )
        sent = (current.astype(jnp.float32) + back).astype(jnp.bfloat16)
        incoming = passed_along(sent, "section", -1)
        return ((incoming, grad_sum), None)

    start_grad = jnp.zeros((width, width), jnp.float32)
    (unused_back, grad_sum), _ = lax.scan(
        backward_step, (start_rows, start_grad), jnp.arange(n_steps, dtype=jnp.int32)
    )
    grad_part = grad_sum.astype(jnp.bfloat16)
    positions = jnp.arange(n_group, dtype=jnp.int32)
    matches = (owner[None, :] == positions[:, None]).astype(jnp.int32)
    blocks_of = jnp.sum(matches * positions[None, :], axis=1)
    flat = saved_in.reshape(n_micro * tok_rows, n_group, block)
    gram_local = jnp.einsum("rbi,rbj->bij", flat, flat, preferred_element_type=jnp.float32)
    gram_ordered = jnp.take(gram_local, blocks_of, axis=0)
    gram_mine = (
        lax.psum_scatter(
            gram_ordered.astype(jnp.bfloat16), "dp", scatter_dimension=0, tiled=True
        ).astype(jnp.float32)
        / total_rows
    )
    gram_out = gram_mine.reshape(1, 1, block, block)
    parts = grad_part.reshape(n_group, block, width)
    ordered = jnp.take(parts, blocks_of, axis=0)
    mine = lax.psum_scatter(ordered, "dp", scatter_dimension=0, tiled=True).astype(jnp.float32)
    rows_mine = jnp.dot(
        preconds[0, 0], mine[0], precision=lax.Precision.HIGHEST, preferred_element_type=jnp.float32
    )
    gathered = lax.all_gather(rows_mine.astype(jnp.bfloat16)[None], "dp", axis=0, tiled=True)
    result = jnp.take(gathered, owner, axis=0).reshape(width, width)
    return (result[None], gram_out)


def solution(mesh):
    placed = (
        P(None, "dp", None),
        P(None, "dp", None),
        P("section", None, None),
        P("section", "dp", None, None),
        P("dp", None),
        P(),
    )
    return jax.shard_map(
        body,
        mesh=mesh,
        in_specs=placed,
        out_specs=(P("section", None, None), P("section", "dp", None, None)),
        check_vma=False,
    )
```

profile of v0, /device:TPU:0, one launch (start us, length us, event | category | flops | bytes accessed | tf_op | source)
XLA Modules:
  0.0 876.2 jit_solution(7326834538762266481)
XLA Ops:
  10.6 2.0 gather_fusion
  12.6 3.2 broadcast_select_fusion.2
  15.8 2.5 broadcast_in_dim.56
  18.3 1.6 broadcast_in_dim.55
  19.9 134.1 %while.30 = (s32[]{:T(128)}, bf16[128,2048]{1,0:T(8,128)(2,1)S(1)}, bf16[4,128,2048]{2,1,0:T(8,128)(2,1)}, f32[4,128,2048]{2,1,0:T(8,128)}, pred[]{:T(512)}, /*i...) while((s32[]{:T(128)}, bf16[128,2048]{1,0:T(8,128)(2,1)S(1)}, ...), condition=%wide.region_1.2_spmd, body=%wide.region_0.1_spmd.sunk | while | flops 1077411840 | bytes 21496572 | solution.py:64
  22.4 2.2 bitcast_dynamic-update-slice_fusion.4
  24.5 5.0 fusion.42
  29.6 1.3 collective-permute-start
  30.9 1.3 constant_dynamic-slice_fusion.5
  35.8 2.2 bitcast_dynamic-update-slice_fusion.4
  37.9 5.0 fusion.42
  43.0 8.0 collective-permute-start
  51.0 1.3 constant_dynamic-slice_fusion.5
  55.8 2.2 bitcast_dynamic-update-slice_fusion.4
  58.0 5.0 fusion.42
  63.0 8.1 collective-permute-start
  71.1 1.3 constant_dynamic-slice_fusion.5
  75.9 2.2 bitcast_dynamic-update-slice_fusion.4
  78.1 5.0 fusion.42
  83.1 8.1 collective-permute-start
  91.2 1.3 constant_dynamic-slice_fusion.5
  96.1 2.2 bitcast_dynamic-update-slice_fusion.4
  98.2 5.0 fusion.42
  103.3 8.1 collective-permute-start
  111.3 1.3 constant_dynamic-slice_fusion.5
  116.2 2.2 bitcast_dynamic-update-slice_fusion.4
  118.3 5.0 fusion.42
  123.4 8.1 collective-permute-start
  131.4 1.3 constant_dynamic-slice_fusion.5
  136.3 2.2 bitcast_dynamic-update-slice_fusion.4
  138.5 5.0 fusion.42
  143.5 8.0 collective-permute-start
  151.5 1.3 constant_dynamic-slice_fusion.5
  154.0 165.9 %while.31 = (s32[]{:T(128)}, bf16[128,2048]{1,0:T(8,128)(2,1)S(1)}, f32[2048,2048]{1,0:T(8,128)}, s32[7]{0:T(128)S(1)}, s32[]{:T(128)}, /*index=5*/pred[]{:T(512...) while((s32[]{:T(128)}, bf16[128,2048]{1,0:T(8,128)(2,1)S(1)}, ...), condition=%wide.region_3.4_spmd.clone, body=%wide.region_2.3_spmd.clone.sunk | while | flops 2168717312 | bytes 51386104 | solution.py:90
  155.3 7.0 fusion.47
  162.4 1.3 collective-permute-start.1
  163.7 9.8 %select_add_fusion.2 = f32[2048,2048]{1,0:T(8,128)} fusion(f32[2048,2048]{1,0:T(8,128)} %get-tuple-element.450, pred[]{:T(512)S(6)} %compare.3, bf16[4,128,2048]{2,1,0:T(8,128)(2,1)} %get-tuple-element.471, s32[]{:T(128)S(6)} %min.14, f32[4,128,2048]{2,1,0:T(8,128)} %get-tuple-element.469, bf16[128,2048]{1,0:T(8,128)(2,1)S(1)} %get-tuple-element.449, ...), kind=kOutput, calls=%fused_computation.18.clone.1 | convolution fusion | flops 1087897600 | bytes 36178432 | tf_op jit(solution)/shard_map/while/body/eval_jaxpr/dot_general | solution.py:79
  174.8 7.0 fusion.47
  181.9 1.3 collective-permute-start.1
  183.2 14.7 %select_add_fusion.2 = f32[2048,2048]{1,0:T(8,128)} fusion(f32[2048,2048]{1,0:T(8,128)} %get-tuple-element.450, pred[]{:T(512)S(6)} %compare.3, bf16[4,128,2048]{2,1,0:T(8,128)(2,1)} %get-tuple-element.471, s32[]{:T(128)S(6)} %min.14, f32[4,128,2048]{2,1,0:T(8,128)} %get-tuple-element.469, bf16[128,2048]{1,0:T(8,128)(2,1)S(1)} %get-tuple-element.449, ...), kind=kOutput, calls=%fused_computation.18.clone.1 | convolution fusion | flops 1087897600 | bytes 36178432 | tf_op jit(solution)/shard_map/while/body/eval_jaxpr/dot_general | solution.py:79
  199.2 7.0 fusion.47
  207.6 14.7 %select_add_fusion.2 = f32[2048,2048]{1,0:T(8,128)} fusion(f32[2048,2048]{1,0:T(8,128)} %get-tuple-element.450, pred[]{:T(512)S(6)} %compare.3, bf16[4,128,2048]{2,1,0:T(8,128)(2,1)} %get-tuple-element.471, s32[]{:T(128)S(6)} %min.14, f32[4,128,2048]{2,1,0:T(8,128)} %get-tuple-element.469, bf16[128,2048]{1,0:T(8,128)(2,1)S(1)} %get-tuple-element.449, ...), kind=kOutput, calls=%fused_computation.18.clone.1 | convolution fusion | flops 1087897600 | bytes 36178432 | tf_op jit(solution)/shard_map/while/body/eval_jaxpr/dot_general | solution.py:79
  223.6 7.0 fusion.47
  230.7 1.3 collective-permute-start.1
  232.0 14.7 %select_add_fusion.2 = f32[2048,2048]{1,0:T(8,128)} fusion(f32[2048,2048]{1,0:T(8,128)} %get-tuple-element.450, pred[]{:T(512)S(6)} %compare.3, bf16[4,128,2048]{2,1,0:T(8,128)(2,1)} %get-tuple-element.471, s32[]{:T(128)S(6)} %min.14, f32[4,128,2048]{2,1,0:T(8,128)} %get-tuple-element.469, bf16[128,2048]{1,0:T(8,128)(2,1)S(1)} %get-tuple-element.449, ...), kind=kOutput, calls=%fused_computation.18.clone.1 | convolution fusion | flops 1087897600 | bytes 36178432 | tf_op jit(solution)/shard_map/while/body/eval_jaxpr/dot_general | solution.py:79
  248.0 7.0 fusion.47
  256.4 14.7 %select_add_fusion.2 = f32[2048,2048]{1,0:T(8,128)} fusion(f32[2048,2048]{1,0:T(8,128)} %get-tuple-element.450, pred[]{:T(512)S(6)} %compare.3, bf16[4,128,2048]{2,1,0:T(8,128)(2,1)} %get-tuple-element.471, s32[]{:T(128)S(6)} %min.14, f32[4,128,2048]{2,1,0:T(8,128)} %get-tuple-element.469, bf16[128,2048]{1,0:T(8,128)(2,1)S(1)} %get-tuple-element.449, ...), kind=kOutput, calls=%fused_computation.18.clone.1 | convolution fusion | flops 1087897600 | bytes 36178432 | tf_op jit(solution)/shard_map/while/body/eval_jaxpr/dot_general | solution.py:79
  272.4 7.0 fusion.47
  280.8 14.7 %select_add_fusion.2 = f32[2048,2048]{1,0:T(8,128)} fusion(f32[2048,2048]{1,0:T(8,128)} %get-tuple-element.450, pred[]{:T(512)S(6)} %compare.3, bf16[4,128,2048]{2,1,0:T(8,128)(2,1)} %get-tuple-element.471, s32[]{:T(128)S(6)} %min.14, f32[4,128,2048]{2,1,0:T(8,128)} %get-tuple-element.469, bf16[128,2048]{1,0:T(8,128)(2,1)S(1)} %get-tuple-element.449, ...), kind=kOutput, calls=%fused_computation.18.clone.1 | convolution fusion | flops 1087897600 | bytes 36178432 | tf_op jit(solution)/shard_map/while/body/eval_jaxpr/dot_general | solution.py:79
  296.8 7.0 fusion.47
  305.2 14.7 %select_add_fusion.2 = f32[2048,2048]{1,0:T(8,128)} fusion(f32[2048,2048]{1,0:T(8,128)} %get-tuple-element.450, pred[]{:T(512)S(6)} %compare.3, bf16[4,128,2048]{2,1,0:T(8,128)(2,1)} %get-tuple-element.471, s32[]{:T(128)S(6)} %min.14, f32[4,128,2048]{2,1,0:T(8,128)} %get-tuple-element.469, bf16[128,2048]{1,0:T(8,128)(2,1)S(1)} %get-tuple-element.449, ...), kind=kOutput, calls=%fused_computation.18.clone.1 | convolution fusion | flops 1087897600 | bytes 36178432 | tf_op jit(solution)/shard_map/while/body/eval_jaxpr/dot_general | solution.py:79
  320.0 9.1 %convert_element_type.41 = bf16[2048,2048]{1,0:T(8,128)(2,1)} convert(f32[2048,2048]{1,0:T(8,128)} %get-tuple-element.195) | non-fusion elementwise | flops 4194304 | bytes 25165824 | tf_op jit(solution)/shard_map/convert_element_type | solution.py:93
  329.1 8.4 gather_fusion.2
  337.5 7.6 broadcast_select_fusion.1
  345.4 1.3 copy-done.2
  346.7 2.6 copy.11
  349.2 2.7 reshape.72
  354.5 212.5 %reduce-scatter.3.cloned.1.call-done = bf16[1,64,2048]{2,1,0:T(8,128)(2,1)} async-done(((bf16[32,64,2048]{2,1,0:T(8,128)(2,1)}), bf16[1,64,2048]{2,1,0:T(8,128)(2,1)}) %reduce-scatter.3.cloned.1.call-update) | async-done | bytes 262160 | tf_op jit(solution)/shard_map/reduce_scatter | solution.py:109
  567.0 2.0 fusion.21
  569.1 182.4 %reduce-scatter.5.cloned.1.call-done = bf16[1,64,64]{2,1,0:T(8,128)(2,1)} async-done(((bf16[32,64,64]{2,1,0:T(8,128)(2,1)}), bf16[1,64,64]{2,1,0:T(8,128)(2,1)}) %reduce-scatter.5.cloned.1.call-update) | async-done | bytes 8208 | tf_op jit(solution)/shard_map/reduce_scatter | solution.py:101
  751.5 1.3 multiply_bitcast_fusion
  752.9 100.5 %all-gather.3.cloned.1.call-done = bf16[2048,2048]{1,0:T(8,128)(2,1)} async-done(((bf16[64,2048]{1,0:T(8,128)(2,1)}), bf16[2048,2048]{1,0:T(8,128)(2,1)}) %all-gather.3.cloned.1.call-update) | async-done | bytes 8388624 | tf_op jit(solution)/shard_map/all_gather | solution.py:113
  853.3 8.6 gather_fusion.3
  861.9 7.8 broadcast_select_fusion
  (96 shorter events, 35.9 us)
Async XLA Ops:
  7.2 3.4 copy-start
  7.2 559.8 %reduce-scatter.3.cloned.1.call-start = ((), (), s32[]{:S(2)}) async-start(), calls=%async_computation.2 | async-start | bytes 8650752 | tf_op jit(solution)/shard_map/reduce_scatter | solution.py:109
  9.5 0.6 copy-start.7
  29.6 3.8 collective-permute-start
  43.0 10.4 %collective-permute-start = (bf16[128,2048]{1,0:T(8,128)(2,1)S(1)}, bf16[128,2048]{1,0:T(8,128)(2,1)S(1)}, u32[]{:S(2)}, u32[]{:S(2)}) collective-permute-start(bf16[128,2048]{1,0:T(8,128)(2,1)S(1)} %get-tuple-element.382), channel_id=1, source_target_pairs={{0,32},{32,64},{64,96},{1,33},{33,65},{65,97},{2,34},{34,66},{66,9... | collective-permute-start | bytes 1572872 | tf_op jit(solution)/shard_map/while/body/eval_jaxpr/ppermute | solution.py:13
  63.0 10.5 %collective-permute-start = (bf16[128,2048]{1,0:T(8,128)(2,1)S(1)}, bf16[128,2048]{1,0:T(8,128)(2,1)S(1)}, u32[]{:S(2)}, u32[]{:S(2)}) collective-permute-start(bf16[128,2048]{1,0:T(8,128)(2,1)S(1)} %get-tuple-element.382), channel_id=1, source_target_pairs={{0,32},{32,64},{64,96},{1,33},{33,65},{65,97},{2,34},{34,66},{66,9... | collective-permute-start | bytes 1572872 | tf_op jit(solution)/shard_map/while/body/eval_jaxpr/ppermute | solution.py:13
  83.1 10.5 %collective-permute-start = (bf16[128,2048]{1,0:T(8,128)(2,1)S(1)}, bf16[128,2048]{1,0:T(8,128)(2,1)S(1)}, u32[]{:S(2)}, u32[]{:S(2)}) collective-permute-start(bf16[128,2048]{1,0:T(8,128)(2,1)S(1)} %get-tuple-element.382), channel_id=1, source_target_pairs={{0,32},{32,64},{64,96},{1,33},{33,65},{65,97},{2,34},{34,66},{66,9... | collective-permute-start | bytes 1572872 | tf_op jit(solution)/shard_map/while/body/eval_jaxpr/ppermute | solution.py:13
  103.3 10.5 %collective-permute-start = (bf16[128,2048]{1,0:T(8,128)(2,1)S(1)}, bf16[128,2048]{1,0:T(8,128)(2,1)S(1)}, u32[]{:S(2)}, u32[]{:S(2)}) collective-permute-start(bf16[128,2048]{1,0:T(8,128)(2,1)S(1)} %get-tuple-element.382), channel_id=1, source_target_pairs={{0,32},{32,64},{64,96},{1,33},{33,65},{65,97},{2,34},{34,66},{66,9... | collective-permute-start | bytes 1572872 | tf_op jit(solution)/shard_map/while/body/eval_jaxpr/ppermute | solution.py:13
  123.4 10.5 %collective-permute-start = (bf16[128,2048]{1,0:T(8,128)(2,1)S(1)}, bf16[128,2048]{1,0:T(8,128)(2,1)S(1)}, u32[]{:S(2)}, u32[]{:S(2)}) collective-permute-start(bf16[128,2048]{1,0:T(8,128)(2,1)S(1)} %get-tuple-element.382), channel_id=1, source_target_pairs={{0,32},{32,64},{64,96},{1,33},{33,65},{65,97},{2,34},{34,66},{66,9... | collective-permute-start | bytes 1572872 | tf_op jit(solution)/shard_map/while/body/eval_jaxpr/ppermute | solution.py:13
  143.5 10.5 %collective-permute-start = (bf16[128,2048]{1,0:T(8,128)(2,1)S(1)}, bf16[128,2048]{1,0:T(8,128)(2,1)S(1)}, u32[]{:S(2)}, u32[]{:S(2)}) collective-permute-start(bf16[128,2048]{1,0:T(8,128)(2,1)S(1)} %get-tuple-element.382), channel_id=1, source_target_pairs={{0,32},{32,64},{64,96},{1,33},{33,65},{65,97},{2,34},{34,66},{66,9... | collective-permute-start | bytes 1572872 | tf_op jit(solution)/shard_map/while/body/eval_jaxpr/ppermute | solution.py:13
  162.4 11.1 %collective-permute-start.1 = (bf16[128,2048]{1,0:T(8,128)(2,1)S(1)}, bf16[128,2048]{1,0:T(8,128)(2,1)S(1)}, u32[]{:S(2)}, u32[]{:S(2)}) collective-permute-start(bf16[128,2048]{1,0:T(8,128)(2,1)S(1)} %fusion.47), channel_id=1, source_target_pairs={{32,0},{64,32},{96,64},{33,1},{65,33},{97,65},{34,2},{66,34},{98,6... | collective-permute-start | bytes 1572872 | tf_op jit(solution)/shard_map/while/body/eval_jaxpr/ppermute | solution.py:13
  181.9 16.0 %collective-permute-start.1 = (bf16[128,2048]{1,0:T(8,128)(2,1)S(1)}, bf16[128,2048]{1,0:T(8,128)(2,1)S(1)}, u32[]{:S(2)}, u32[]{:S(2)}) collective-permute-start(bf16[128,2048]{1,0:T(8,128)(2,1)S(1)} %fusion.47), channel_id=1, source_target_pairs={{32,0},{64,32},{96,64},{33,1},{65,33},{97,65},{34,2},{66,34},{98,6... | collective-permute-start | bytes 1572872 | tf_op jit(solution)/shard_map/while/body/eval_jaxpr/ppermute | solution.py:13
  206.3 16.0 %collective-permute-start.1 = (bf16[128,2048]{1,0:T(8,128)(2,1)S(1)}, bf16[128,2048]{1,0:T(8,128)(2,1)S(1)}, u32[]{:S(2)}, u32[]{:S(2)}) collective-permute-start(bf16[128,2048]{1,0:T(8,128)(2,1)S(1)} %fusion.47), channel_id=1, source_target_pairs={{32,0},{64,32},{96,64},{33,1},{65,33},{97,65},{34,2},{66,34},{98,6... | collective-permute-start | bytes 1572872 | tf_op jit(solution)/shard_map/while/body/eval_jaxpr/ppermute | solution.py:13
  230.7 16.0 %collective-permute-start.1 = (bf16[128,2048]{1,0:T(8,128)(2,1)S(1)}, bf16[128,2048]{1,0:T(8,128)(2,1)S(1)}, u32[]{:S(2)}, u32[]{:S(2)}) collective-permute-start(bf16[128,2048]{1,0:T(8,128)(2,1)S(1)} %fusion.47), channel_id=1, source_target_pairs={{32,0},{64,32},{96,64},{33,1},{65,33},{97,65},{34,2},{66,34},{98,6... | collective-permute-start | bytes 1572872 | tf_op jit(solution)/shard_map/while/body/eval_jaxpr/ppermute | solution.py:13
  255.1 16.0 %collective-permute-start.1 = (bf16[128,2048]{1,0:T(8,128)(2,1)S(1)}, bf16[128,2048]{1,0:T(8,128)(2,1)S(1)}, u32[]{:S(2)}, u32[]{:S(2)}) collective-permute-start(bf16[128,2048]{1,0:T(8,128)(2,1)S(1)} %fusion.47), channel_id=1, source_target_pairs={{32,0},{64,32},{96,64},{33,1},{65,33},{97,65},{34,2},{66,34},{98,6... | collective-permute-start | bytes 1572872 | tf_op jit(solution)/shard_map/while/body/eval_jaxpr/ppermute | solution.py:13
  279.5 16.0 %collective-permute-start.1 = (bf16[128,2048]{1,0:T(8,128)(2,1)S(1)}, bf16[128,2048]{1,0:T(8,128)(2,1)S(1)}, u32[]{:S(2)}, u32[]{:S(2)}) collective-permute-start(bf16[128,2048]{1,0:T(8,128)(2,1)S(1)} %fusion.47), channel_id=1, source_target_pairs={{32,0},{64,32},{96,64},{33,1},{65,33},{97,65},{34,2},{66,34},{98,6... | collective-permute-start | bytes 1572872 | tf_op jit(solution)/shard_map/while/body/eval_jaxpr/ppermute | solution.py:13
  303.9 16.0 %collective-permute-start.1 = (bf16[128,2048]{1,0:T(8,128)(2,1)S(1)}, bf16[128,2048]{1,0:T(8,128)(2,1)S(1)}, u32[]{:S(2)}, u32[]{:S(2)}) collective-permute-start(bf16[128,2048]{1,0:T(8,128)(2,1)S(1)} %fusion.47), channel_id=1, source_target_pairs={{32,0},{64,32},{96,64},{33,1},{65,33},{97,65},{34,2},{66,34},{98,6... | collective-permute-start | bytes 1572872 | tf_op jit(solution)/shard_map/while/body/eval_jaxpr/ppermute | solution.py:13
  320.0 9.1 %copy-start.5 = (s32[32]{0:T(128)S(1)}, s32[32]{0:T(128)}, u32[]{:S(2)}) copy-start(s32[32]{0:T(128)} %compare_select_fusion.1) | copy-start | bytes 388
  329.0 8.4 copy-start.4
  345.1 1.6 copy-start.2
  345.1 6.9 copy-start.8
  345.1 406.4 %reduce-scatter.5.cloned.1.call-start = ((), (), s32[]{:S(2)}) async-start(), calls=%async_computation.3 | async-start | bytes 540672 | tf_op jit(solution)/shard_map/reduce_scatter | solution.py:101
  352.0 215.0 %copy-start.3 = (f32[1,1,64,64]{3,2,1,0:T(8,128)S(1)}, f32[1,1,64,64]{3,2,1,0:T(8,128)}, u32[]{:S(2)}) copy-start(f32[1,1,64,64]{3,2,1,0:T(8,128)} %param.15) | copy-start | bytes 49156
  352.0 217.0 %copy-start.6 = (s32[32]{0:T(128)S(1)}, s32[32]{0:T(128)}, u32[]{:S(2)}) copy-start(s32[32]{0:T(128)} %param.17) | copy-start | bytes 388
  354.4 498.9 %all-gather.3.cloned.1.call-start = ((), (), s32[]{:S(2)}) async-start(), calls=%async_computation.4 | async-start | bytes 8650752 | tf_op jit(solution)/shard_map/all_gather | solution.py:113
  861.9 7.8 copy-start.1
Sparse Core Ops, SparseCore 0:
  345.2 221.7 reduce-scatter.2
  569.3 182.1 reduce-scatter.4
  755.1 98.1 all-gather.2
where the time goes:
time: 878 us; the launch traced here: 876 us
  waiting for transfers between devices  495 us (56%)
  matrix products  185 us (21%)
  starting transfers between devices  58.9 us (7%)
  local copies, waits for them, and re-layouts  56.4 us (6%)
  other arithmetic  56.3 us (6%)
  between operations  13.9 us (2%)
  loops' own time  9.9 us (1%)
    reduce_scatter x1, waiting for transfers between devices, body(): lax.psum_scatter(ordered, 'dp', scatter_dimension=0, tiled=True)  213 us
    reduce_scatter x1, waiting for transfers between devices, body(): lax.psum_scatter(gram_ordered.astype(jnp.bfloat16), 'dp', scatter_dimensi...  182 us
    all_gather x1, waiting for transfers between devices, body(): lax.all_gather(rows_mine.astype(jnp.bfloat16)[None], 'dp', axis=0, tiled=...  100 us
    dot_general x7, matrix products, backward_step(): lax.dot_general(acts, slopes, (((0,), (0,)), ((), ())), preferred_element...  98.1 us
    ppermute x14, starting transfers between devices, passed_along(): return lax.ppermute(block, axis, route)  58.6 us
    dot_general x7, matrix products, backward_step(): lax.dot_general(slopes, weight, (((1,), (1,)), ((), ())), preferred_eleme...  49.3 us
    dot_general x7, matrix products, forward_step(): pre = jnp.dot(current, weight, preferred_element_type=jnp.float32)  35.2 us
  transfers between devices with their start and end apart: 17, of which 3 were waited for; matrix products, arithmetic and copies ran while one was open for 14% of the time, Pallas kernels for 0%

commit v1 on v0

--- a/solution.py
+++ b/solution.py
@@ -1,7 +1,13 @@
+import functools
+
 import jax
 import jax.numpy as jnp
 from jax import lax
+from jax.experimental import pallas as pl
+from jax.experimental.pallas import tpu as pltpu
 from jax.sharding import PartitionSpec as P
+
+MESH = pl.DeviceIdType.MESH
 
 coef = 0.7978845608028654
 cubic = 0.044715
@@ -23,6 +29,378 @@
     return 0.5 * (1.0 + tanh_part) + 0.5 * z * (1.0 - tanh_part * tanh_part) * coef * (
         1.0 + 3.0 * cubic * z * z
     )
+
+
+WIDE = 512
+STAGES = 11
+
+
+def dp_kernel(
+    kinds,
+    order,
+    blocks_ref,
+    h_ref,
+    dz_ref,
+    pc_ref,
+    out_ref,
+    gram_ref,
+    h_t,
+    h_p,
+    part,
+    from1,
+    part2,
+    from2,
+    last,
+    from3,
+    full,
+    g_part,
+    g_from1,
+    g_part2,
+    g_from2,
+    g_last,
+    g_from3,
+    send1,
+    recv1,
+    send2,
+    recv2,
+    send3,
+    recv3,
+    send4,
+    recv4,
+    out_sem,
+):
+    n_chunks = len(kinds)
+    me = lax.axis_index("dp")
+    my_z, my_x, my_y = me // 8, (me // 2) % 4, me % 2
+
+    def place(z, x, y):
+        return z * 8 + x * 2 + y
+
+    rings = {}
+    for name, mine in (("x", my_x), ("z", my_z)):
+        up, down, far = (mine + 1) % 4, (mine + 3) % 4, (mine + 2) % 4
+        if name == "x":
+            dev_up, dev_down = place(my_z, up, my_y), place(my_z, down, my_y)
+        else:
+            dev_up, dev_down = place(up, my_x, my_y), place(down, my_x, my_y)
+        rings[name] = (mine, up, down, far, dev_up, dev_down)
+    mate = place(my_z, my_x, 1 - my_y)
+
+    barrier = pltpu.get_barrier_semaphore()
+    for dev in (rings["x"][4], rings["x"][5], rings["z"][4], rings["z"][5], mate):
+        pl.semaphore_signal(barrier, inc=1, device_id={"dp": dev}, device_id_type=MESH)
+
+    def remote(src, dst, send, recv, dev):
+        return pltpu.make_async_remote_copy(
+            src_ref=src, dst_ref=dst, send_sem=send, recv_sem=recv, device_id={"dp": dev}, device_id_type=MESH
+        )
+
+    rows = h_ref.shape[0]
+    for tile in range(8):
+        block = h_ref[:, tile * 256 : (tile + 1) * 256].T
+        h_t[tile * 4 : (tile + 1) * 4] = block.reshape(4, 64, rows)
+
+    def move(p, carry):
+        h_p[p // 8, (p // 2) % 4, p % 2] = h_t[blocks_ref[p]]
+        return carry
+
+    lax.fori_loop(0, 32, move, 0)
+
+    sent = []
+
+    def start(copy):
+        copy.start()
+        sent.append(copy)
+        return copy
+
+    class Chunk:
+        def __init__(self, slot, kind, bufs):
+            first, second = ("x", "z") if kind == 0 else ("z", "x")
+            self.slot, self.kind = slot, kind
+            self.r1, self.r2 = rings[first], rings[second]
+            self.part, self.from1, self.part2, self.from2, self.last, self.from3 = bufs
+            self.c = {}
+
+        def ring_sends(self, stage, part, landed, send, recv, ring, names):
+            mine, up, down, far, dev_up, dev_down = ring
+            table = {
+                "mp": (far, 0, 0, dev_up),
+                "mm": (far, 1, 1, dev_down),
+                "dp": (up, 1, 2, dev_up),
+                "dm": (down, 0, 3, dev_down),
+                "tp": (up, 0, 4, dev_up),
+                "tm": (down, 1, 5, dev_down),
+            }
+            for name in names:
+                r, y, k, dev = table[name]
+                self.c[stage, name] = start(
+                    remote(part.at[r, y], landed.at[k], send.at[self.slot, k], recv.at[self.slot, k], dev)
+                )
+
+        def add_far(self, stage, part, landed, ring):
+            mine, up, down, far, dev_up, dev_down = ring
+            for name, r, y, k in (("mp", up, 0, 0), ("mm", down, 1, 1)):
+                self.c[stage, name].wait_recv()
+                total = part[r, y].astype(jnp.float32) + landed[k].astype(jnp.float32)
+                part[r, y] = total.astype(jnp.bfloat16)
+
+        def sums(self, stage, part, landed, ring):
+            for name in ("dp", "dm", "tp", "tm"):
+                self.c[stage, name].wait_recv()
+            mine = ring[0]
+            for y, a, b in ((0, 3, 4), (1, 2, 5)):
+                yield y, (
+                    part[mine, y].astype(jnp.float32)
+                    + landed[a].astype(jnp.float32)
+                    + landed[b].astype(jnp.float32)
+                )
+
+        def run(self, stage):
+            return getattr(self, f"stage{stage}")()
+
+        def product(self, r, y):
+            cols = slice(self.slot * WIDE, (self.slot + 1) * WIDE)
+            left = h_p[:, r, y] if self.kind == 0 else h_p[r, :, y]
+            value = jnp.dot(left.reshape(256, rows), dz_ref[:, cols], preferred_element_type=jnp.float32)
+            self.part[r, y] = value.astype(jnp.bfloat16).reshape(4, 64, WIDE)
+
+        def stage0(self):
+            mine, up, down, far = self.r1[:4]
+            args = (1, self.part, self.from1, send1, recv1, self.r1)
+            self.product(far, 0)
+            self.ring_sends(*args, ("mp",))
+            self.product(far, 1)
+            self.ring_sends(*args, ("mm",))
+            self.product(up, 1)
+            self.ring_sends(*args, ("dp",))
+            self.product(down, 0)
+            self.ring_sends(*args, ("dm",))
+            self.product(up, 0)
+            self.product(down, 1)
+
+        def stage1(self):
+            self.add_far(1, self.part, self.from1, self.r1)
+            self.ring_sends(1, self.part, self.from1, send1, recv1, self.r1, ("tp", "tm"))
+            self.product(self.r1[0], 0)
+            self.product(self.r1[0], 1)
+
+        def stage2(self):
+            for y, total in self.sums(1, self.part, self.from1, self.r1):
+                for r in range(4):
+                    self.part2[r, y] = total[r].astype(jnp.bfloat16)
+            self.ring_sends(2, self.part2, self.from2, send2, recv2, self.r2, ("mp", "mm", "dp", "dm"))
+
+        def stage3(self):
+            self.add_far(2, self.part2, self.from2, self.r2)
+            self.ring_sends(2, self.part2, self.from2, send2, recv2, self.r2, ("tp", "tm"))
+
+        def stage4(self):
+            for y, total in self.sums(2, self.part2, self.from2, self.r2):
+                self.last[y] = total.astype(jnp.bfloat16)
+            self.c["y"] = start(
+                remote(self.last.at[1 - my_y], self.from3, send3.at[self.slot], recv3.at[self.slot], mate)
+            )
+
+        def total(self):
+            self.c["y"].wait_recv()
+            return self.last[my_y].astype(jnp.float32) + self.from3[...].astype(jnp.float32)
+
+        def gather(self, name, k, where, dev):
+            ref = full.at[self.slot].at[where]
+            self.c["g", name] = start(
+                remote(ref, ref, send4.at[self.slot, k], recv4.at[self.slot, k], dev)
+            )
+
+        def stage5(self):
+            done = jnp.dot(
+                pc_ref[...], self.total(), precision=lax.Precision.HIGHEST, preferred_element_type=jnp.float32
+            )
+            m1, m2 = self.r1[0], self.r2[0]
+            full[self.slot, m1, m2, my_y] = done.astype(jnp.bfloat16)
+            self.gather("y", 0, (m1, m2, my_y), mate)
+
+        def stage6(self):
+            self.c["g", "y"].wait_recv()
+            m1, m2 = self.r1[0], self.r2[0]
+            self.gather("2p", 1, (m1, m2), self.r2[4])
+            self.gather("2m", 2, (m1, m2), self.r2[5])
+
+        def stage7(self):
+            m1 = self.r1[0]
+            self.c["g", "2p"].wait_recv()
+            self.gather("f2p", 3, (m1, self.r2[2], 0), self.r2[4])
+            self.c["g", "2m"].wait_recv()
+            self.gather("f2m", 4, (m1, self.r2[1], 1), self.r2[5])
+
+        def stage8(self):
+            self.c["g", "f2p"].wait_recv()
+            self.c["g", "f2m"].wait_recv()
+            self.gather("1p", 5, (self.r1[0],), self.r1[4])
+            self.gather("1m", 6, (self.r1[0],), self.r1[5])
+
+        def stage9(self):
+            self.c["g", "1p"].wait_recv()
+            self.gather("f1p", 7, (self.r1[2], slice(None), 0), self.r1[4])
+            self.c["g", "1m"].wait_recv()
+            self.gather("f1m", 8, (self.r1[1], slice(None), 1), self.r1[5])
+
+        def stage10(self):
+            self.c["g", "f1p"].wait_recv()
+            self.c["g", "f1m"].wait_recv()
+            copy = pltpu.make_async_copy(full.at[self.slot], out_ref.at[self.slot], out_sem.at[self.slot])
+            copy.start()
+            self.out = copy
+
+    g_part[...] = jnp.zeros(g_part.shape, g_part.dtype)
+    for z in range(4):
+        for half in range(2):
+            left = h_p[z, half * 2 : half * 2 + 2].reshape(256, rows)
+            square = lax.dot_general(left, left, (((1,), (1,)), ((), ())), preferred_element_type=jnp.float32)
+            for k in range(4):
+                lanes = slice(k * 64, (k + 1) * 64)
+                g_part[half * 2 + k // 2, k % 2, z, :, 0:64] = square[lanes, lanes].astype(jnp.bfloat16)
+    pl.semaphore_wait(barrier, 5)
+
+    g_bufs = (g_part, g_from1, g_part2, g_from2, g_last, g_from3)
+    gram = Chunk(n_chunks, 0, g_bufs)
+    gram.ring_sends(1, g_part, g_from1, send1, recv1, gram.r1, ("mp", "mm", "dp", "dm"))
+
+    def gram_stage1():
+        gram.add_far(1, g_part, g_from1, gram.r1)
+        gram.ring_sends(1, g_part, g_from1, send1, recv1, gram.r1, ("tp", "tm"))
+
+    def gram_stage5():
+        gram_ref[...] = gram.total()[:, 0:64] * (1.0 / 16384.0)
+
+    gram_stages = {1: gram_stage1, 2: gram.stage2, 3: gram.stage3, 4: gram.stage4, 5: gram_stage5}
+    chunks = []
+    for slot, kind in enumerate(kinds):
+        bufs = tuple(ref.at[slot] for ref in (part, from1, part2, from2, last, from3))
+        chunks.append(Chunk(slot, kind, bufs))
+    for slot, stage in order:
+        if slot == n_chunks:
+            gram_stages[stage]()
+        else:
+            chunks[slot].run(stage)
+    for copy in sent:
+        copy.wait_send()
+    for chunk in chunks:
+        chunk.out.wait()
+
+
+def dp_order(n_chunks, lag):
+    order = []
+    for step in range(STAGES + lag * (n_chunks // 2 - 1)):
+        for slot in range(n_chunks):
+            stage = step - lag * (slot // 2)
+            if 0 <= stage < STAGES:
+                order.append((slot, stage))
+        if 0 <= step < 5:
+            order.append((n_chunks, step + 1))
+    return tuple(order)
+
+
+KINDS = (0, 1, 0, 1)
+LAG = 2
+
+
+def dp_part(acts, slopes, precond, blocks_of):
+    n = len(KINDS)
+    rows, width = acts.shape
+    bf = jnp.bfloat16
+    vmem = pl.BlockSpec(memory_space=pltpu.VMEM)
+
+    def ring_scratch(lead, wide):
+        return [
+            pltpu.VMEM((*lead, 4, 2, 4, 64, wide), bf),
+            pltpu.VMEM((*lead, 6, 4, 64, wide), bf),
+            pltpu.VMEM((*lead, 4, 2, 64, wide), bf),
+            pltpu.VMEM((*lead, 6, 64, wide), bf),
+            pltpu.VMEM((*lead, 2, 64, wide), bf),
+            pltpu.VMEM((*lead, 64, wide), bf),
+        ]
+
+    dma = pltpu.SemaphoreType.DMA
+    return pl.pallas_call(
+        functools.partial(dp_kernel, KINDS, dp_order(n, LAG)),
+        out_shape=(
+            jax.ShapeDtypeStruct((n, 4, 4, 2, 64, WIDE), bf),
+            jax.ShapeDtypeStruct((64, 64), jnp.float32),
+        ),
+        in_specs=[pl.BlockSpec(memory_space=pltpu.SMEM), vmem, vmem, vmem],
+        out_specs=(pl.BlockSpec(memory_space=pl.ANY), vmem),
+        scratch_shapes=[
+            pltpu.VMEM((32, 64, rows), bf),
+            pltpu.VMEM((4, 4, 2, 64, rows), bf),
+            *ring_scratch((n,), WIDE),
+            pltpu.VMEM((n, 4, 4, 2, 64, WIDE), bf),
+            *ring_scratch((), 128),
+            dma((n + 1, 6)),
+            dma((n + 1, 6)),
+            dma((n + 1, 6)),
+            dma((n + 1, 6)),
+            dma((n + 1,)),
+            dma((n + 1,)),
+            dma((n, 9)),
+            dma((n, 9)),
+            dma((n,)),
+        ],
+        compiler_params=pltpu.CompilerParams(
+            collective_id=1, has_side_effects=True, vmem_limit_bytes=60 * 1024 * 1024
+        ),
+        name="dp_part",
+    )(blocks_of, acts, slopes, precond)
+
+
+def restore_kernel(owner_ref, src_ref, dst_ref, held, in_sem, out_sem):
+    n = len(KINDS)
+
+    def fetch(b, c):
+        o = owner_ref[b]
+        z, x, y = o // 8, (o // 2) % 4, o % 2
+        where = (x, z, y) if KINDS[c] == 0 else (z, x, y)
+        return pltpu.make_async_copy(
+            src_ref.at[(c, *where)], held.at[b, :, pl.ds(c * WIDE, WIDE)], in_sem.at[b, c]
+        )
+
+    def first(b, carry):
+        for c in range(n):
+            fetch(b, c).start()
+        return carry
+
+    def put(b):
+        return pltpu.make_async_copy(held.at[b], dst_ref.at[b], out_sem.at[b])
+
+    def second(b, carry):
+        for c in range(n):
+            fetch(b, c).wait()
+        put(b).start()
+        return carry
+
+    def third(b, carry):
+        put(b).wait()
+        return carry
+
+    lax.fori_loop(0, 32, first, 0)
+    lax.fori_loop(0, 32, second, 0)
+    lax.fori_loop(0, 32, third, 0)
+
+
+def restore(gathered, owner):
+    n = len(KINDS)
+    return pl.pallas_call(
+        restore_kernel,
+        out_shape=jax.ShapeDtypeStruct((32, 64, n * WIDE), jnp.bfloat16),
+        in_specs=[pl.BlockSpec(memory_space=pltpu.SMEM), pl.BlockSpec(memory_space=pl.ANY)],
+        out_specs=pl.BlockSpec(memory_space=pl.ANY),
+        scratch_shapes=[
+            pltpu.VMEM((32, 64, n * WIDE), jnp.bfloat16),
+            pltpu.SemaphoreType.DMA((32, n)),
+            pltpu.SemaphoreType.DMA((32,)),
+        ],
+        compiler_params=pltpu.CompilerParams(vmem_limit_bytes=40 * 1024 * 1024),
+        name="restore",
+    )(owner, gathered)
 
 
 def body(inputs, cotangent, weights, preconds, order, owner):
@@ -66,7 +444,7 @@
     )
 
     def backward_step(carry, step):
-        incoming, grad_sum = carry
+        incoming, kept = carry
         slot = step - (sections - 1 - place)
         valid = (slot >= 0) & (slot < n_micro)
         slot_c = jnp.clip(slot, 0, n_micro - 1)
@@ -76,43 +454,27 @@
         acts = lax.dynamic_index_in_dim(saved_in, slot_c, 0, keepdims=False)
         pre = lax.dynamic_index_in_dim(saved_pre, slot_c, 0, keepdims=False)
         slopes = (current.astype(jnp.float32) * gelu_slope(pre)).astype(jnp.bfloat16)
-        grad_sum = grad_sum + lax.dot_general(
-            acts, slopes, (((0,), (0,)), ((), ())), preferred_element_type=jnp.float32
-        )
+        old = lax.dynamic_index_in_dim(kept, slot_c, 0, keepdims=False)
+        kept = lax.dynamic_update_index_in_dim(kept, jnp.where(valid, slopes, old), slot_c, 0)
         back = lax.dot_general(
             slopes, weight, (((1,), (1,)), ((), ())), preferred_element_type=jnp.float32
         )
         sent = (current.astype(jnp.float32) + back).astype(jnp.bfloat16)
         incoming = passed_along(sent, "section", -1)
-        return ((incoming, grad_sum), None)
-
-    start_grad = jnp.zeros((width, width), jnp.float32)
-    (unused_back, grad_sum), _ = lax.scan(
-        backward_step, (start_rows, start_grad), jnp.arange(n_steps, dtype=jnp.int32)
-    )
-    grad_part = grad_sum.astype(jnp.bfloat16)
+        return ((incoming, kept), None)
+
+    kept = jnp.zeros_like(saved_in)
+    (unused_back, kept), _ = lax.scan(
+        backward_step, (start_rows, kept), jnp.arange(n_steps, dtype=jnp.int32)
+    )
     positions = jnp.arange(n_group, dtype=jnp.int32)
     matches = (owner[None, :] == positions[:, None]).astype(jnp.int32)
     blocks_of = jnp.sum(matches * positions[None, :], axis=1)
-    flat = saved_in.reshape(n_micro * tok_rows, n_group, block)
-    gram_local = jnp.einsum("rbi,rbj->bij", flat, flat, preferred_element_type=jnp.float32)
-    gram_ordered = jnp.take(gram_local, blocks_of, axis=0)
-    gram_mine = (
-        lax.psum_scatter(
-            gram_ordered.astype(jnp.bfloat16), "dp", scatter_dimension=0, tiled=True
-        ).astype(jnp.float32)
-        / total_rows
-    )
-    gram_out = gram_mine.reshape(1, 1, block, block)
-    parts = grad_part.reshape(n_group, block, width)
-    ordered = jnp.take(parts, blocks_of, axis=0)
-    mine = lax.psum_scatter(ordered, "dp", scatter_dimension=0, tiled=True).astype(jnp.float32)
-    rows_mine = jnp.dot(
-        preconds[0, 0], mine[0], precision=lax.Precision.HIGHEST, preferred_element_type=jnp.float32
-    )
-    gathered = lax.all_gather(rows_mine.astype(jnp.bfloat16)[None], "dp", axis=0, tiled=True)
-    result = jnp.take(gathered, owner, axis=0).reshape(width, width)
-    return (result[None], gram_out)
+    gathered, gram = dp_part(
+        saved_in.reshape(-1, width), kept.reshape(-1, width), preconds[0, 0], blocks_of
+    )
+    result = restore(gathered, owner).reshape(1, width, width)
+    return (result, gram.reshape(1, 1, block, block))
 
 
 def solution(mesh):

time: 878 us -> 438 us (0.50)
  the two profiles are of different devices: /device:TPU:0 before, /device:TPU:8 now
where the time goes in v1:
time: 438 us; the launch traced here: 435 us
  Pallas kernels  119 us (27%)
  matrix products  98.6 us (23%)
  waiting for transfers between devices  60.6 us (14%)
  other arithmetic  54.5 us (12%)
  local copies, waits for them, and re-layouts  54 us (12%)
  starting transfers between devices  38.1 us (9%)
  loops' own time  9.66 us (2%)
    pallas_call x1, Pallas kernels, dp_part(): pl.pallas_call(functools.partial(dp_kernel, KINDS, dp_order(n, LAG)), out...  110 us
    ppermute x14, waiting for transfers between devices, passed_along(): return lax.ppermute(block, axis, route)  60.6 us
    dot_general x7, matrix products, backward_step(): lax.dot_general(slopes, weight, (((1,), (1,)), ((), ())), preferred_eleme...  55.4 us
    dot_general x7, matrix products, forward_step(): pre = jnp.dot(current, weight, preferred_element_type=jnp.float32)  43.2 us
    ppermute x14, starting transfers between devices, passed_along(): return lax.ppermute(block, axis, route)  38.1 us
    dynamic_update_slice x7, other arithmetic, backward_step(): lax.dynamic_update_index_in_dim(kept, jnp.where(valid, slopes, old), slot...  21.2 us
    dynamic_update_slice x7, other arithmetic, forward_step(): lax.dynamic_update_index_in_dim(kept_in, jnp.where(valid, current, old_in...  16.1 us
    dynamic_update_slice x7, other arithmetic, forward_step(): lax.dynamic_update_index_in_dim(kept_pre, jnp.where(valid, pre, old_pre),...  12.6 us
  transfers between devices with their start and end apart: 14, of which 14 were waited for; matrix products, arithmetic and copies ran while one was open for 12% of the time, Pallas kernels for 0%

profile of v1, /device:TPU:8, one launch (start us, length us, event | category | flops | bytes accessed | tf_op | source)
XLA Modules:
  0.0 434.8 jit_solution(5702641273467206811)
XLA Ops:
  2.2 2.0 gather_fusion
  4.3 3.2 broadcast_select_fusion
  7.4 2.5 broadcast_in_dim.31
  12.4 152.1 %while.29 = (s32[]{:T(128)}, bf16[128,2048]{1,0:T(8,128)(2,1)}, bf16[4,128,2048]{2,1,0:T(8,128)(2,1)}, f32[4,128,2048]{2,1,0:T(8,128)}, pred[]{:T(512)}, /*index...) while((s32[]{:T(128)}, bf16[128,2048]{1,0:T(8,128)(2,1)}, ...), condition=%wide.region_2.3_spmd, body=%wide.region_1.2_spmd.sunk | while | flops 1077411840 | bytes 21496572 | solution.py:442
  14.9 2.3 bitcast_dynamic-update-slice_fusion.6
  17.2 6.2 %fusion.29 = (bf16[128,2048]{1,0:T(8,128)(2,1)}, f32[128,2048]{1,0:T(8,128)}) fusion(bf16[128,2048]{1,0:T(8,128)(2,1)S(1)} %get-tuple-element.333, bf16[2048,2048]{1,0:T(8,128)(2,1)} %get-tuple-element.380), kind=kOutput, calls=%fused_computation.7.clone.1 | convolution fusion | flops 1076625408 | bytes 10485760 | tf_op jit(solution)/shard_map/while/body/eval_jaxpr/dot_general | solution.py:428
  23.4 1.9 collective-permute-start
  27.7 6.5 %collective-permute-done = bf16[128,2048]{1,0:T(8,128)(2,1)} collective-permute-done((bf16[128,2048]{1,0:T(8,128)(2,1)}, bf16[128,2048]{1,0:T(8,128)(2,1)}, u32[]{:S(2)}, u32[]{:S(2)}) %collective-permute-start) | collective-permute-done | bytes 524320 | tf_op jit(solution)/shard_map/while/body/eval_jaxpr/ppermute | solution.py:19
  36.6 2.3 bitcast_dynamic-update-slice_fusion.6
  39.0 6.2 %fusion.29 = (bf16[128,2048]{1,0:T(8,128)(2,1)}, f32[128,2048]{1,0:T(8,128)}) fusion(bf16[128,2048]{1,0:T(8,128)(2,1)S(1)} %get-tuple-element.333, bf16[2048,2048]{1,0:T(8,128)(2,1)} %get-tuple-element.380), kind=kOutput, calls=%fused_computation.7.clone.1 | convolution fusion | flops 1076625408 | bytes 10485760 | tf_op jit(solution)/shard_map/while/body/eval_jaxpr/dot_general | solution.py:428
  45.1 1.9 collective-permute-start
  49.5 6.5 %collective-permute-done = bf16[128,2048]{1,0:T(8,128)(2,1)} collective-permute-done((bf16[128,2048]{1,0:T(8,128)(2,1)}, bf16[128,2048]{1,0:T(8,128)(2,1)}, u32[]{:S(2)}, u32[]{:S(2)}) %collective-permute-start) | collective-permute-done | bytes 524320 | tf_op jit(solution)/shard_map/while/body/eval_jaxpr/ppermute | solution.py:19
  58.4 2.3 bitcast_dynamic-update-slice_fusion.6
  60.7 6.2 %fusion.29 = (bf16[128,2048]{1,0:T(8,128)(2,1)}, f32[128,2048]{1,0:T(8,128)}) fusion(bf16[128,2048]{1,0:T(8,128)(2,1)S(1)} %get-tuple-element.333, bf16[2048,2048]{1,0:T(8,128)(2,1)} %get-tuple-element.380), kind=kOutput, calls=%fused_computation.7.clone.1 | convolution fusion | flops 1076625408 | bytes 10485760 | tf_op jit(solution)/shard_map/while/body/eval_jaxpr/dot_general | solution.py:428
  66.9 1.9 collective-permute-start
  70.1 2.3 bitcast_dynamic-update-slice_fusion.7
  72.4 5.3 %collective-permute-done = bf16[128,2048]{1,0:T(8,128)(2,1)} collective-permute-done((bf16[128,2048]{1,0:T(8,128)(2,1)}, bf16[128,2048]{1,0:T(8,128)(2,1)}, u32[]{:S(2)}, u32[]{:S(2)}) %collective-permute-start) | collective-permute-done | bytes 524320 | tf_op jit(solution)/shard_map/while/body/eval_jaxpr/ppermute | solution.py:19
  80.1 2.3 bitcast_dynamic-update-slice_fusion.6
  82.5 6.2 %fusion.29 = (bf16[128,2048]{1,0:T(8,128)(2,1)}, f32[128,2048]{1,0:T(8,128)}) fusion(bf16[128,2048]{1,0:T(8,128)(2,1)S(1)} %get-tuple-element.333, bf16[2048,2048]{1,0:T(8,128)(2,1)} %get-tuple-element.380), kind=kOutput, calls=%fused_computation.7.clone.1 | convolution fusion | flops 1076625408 | bytes 10485760 | tf_op jit(solution)/shard_map/while/body/eval_jaxpr/dot_general | solution.py:428
  88.6 1.9 collective-permute-start
  91.9 2.3 bitcast_dynamic-update-slice_fusion.7
  94.2 5.3 %collective-permute-done = bf16[128,2048]{1,0:T(8,128)(2,1)} collective-permute-done((bf16[128,2048]{1,0:T(8,128)(2,1)}, bf16[128,2048]{1,0:T(8,128)(2,1)}, u32[]{:S(2)}, u32[]{:S(2)}) %collective-permute-start) | collective-permute-done | bytes 524320 | tf_op jit(solution)/shard_map/while/body/eval_jaxpr/ppermute | solution.py:19
  101.9 2.3 bitcast_dynamic-update-slice_fusion.6
  104.2 6.2 %fusion.29 = (bf16[128,2048]{1,0:T(8,128)(2,1)}, f32[128,2048]{1,0:T(8,128)}) fusion(bf16[128,2048]{1,0:T(8,128)(2,1)S(1)} %get-tuple-element.333, bf16[2048,2048]{1,0:T(8,128)(2,1)} %get-tuple-element.380), kind=kOutput, calls=%fused_computation.7.clone.1 | convolution fusion | flops 1076625408 | bytes 10485760 | tf_op jit(solution)/shard_map/while/body/eval_jaxpr/dot_general | solution.py:428
  113.6 2.3 bitcast_dynamic-update-slice_fusion.7
  115.9 5.3 %collective-permute-done = bf16[128,2048]{1,0:T(8,128)(2,1)} collective-permute-done((bf16[128,2048]{1,0:T(8,128)(2,1)}, bf16[128,2048]{1,0:T(8,128)(2,1)}, u32[]{:S(2)}, u32[]{:S(2)}) %collective-permute-start) | collective-permute-done | bytes 524320 | tf_op jit(solution)/shard_map/while/body/eval_jaxpr/ppermute | solution.py:19
  123.6 2.3 bitcast_dynamic-update-slice_fusion.6
  125.9 6.2 %fusion.29 = (bf16[128,2048]{1,0:T(8,128)(2,1)}, f32[128,2048]{1,0:T(8,128)}) fusion(bf16[128,2048]{1,0:T(8,128)(2,1)S(1)} %get-tuple-element.333, bf16[2048,2048]{1,0:T(8,128)(2,1)} %get-tuple-element.380), kind=kOutput, calls=%fused_computation.7.clone.1 | convolution fusion | flops 1076625408 | bytes 10485760 | tf_op jit(solution)/shard_map/while/body/eval_jaxpr/dot_general | solution.py:428
  135.3 2.3 bitcast_dynamic-update-slice_fusion.7
  137.6 5.3 %collective-permute-done = bf16[128,2048]{1,0:T(8,128)(2,1)} collective-permute-done((bf16[128,2048]{1,0:T(8,128)(2,1)}, bf16[128,2048]{1,0:T(8,128)(2,1)}, u32[]{:S(2)}, u32[]{:S(2)}) %collective-permute-start) | collective-permute-done | bytes 524320 | tf_op jit(solution)/shard_map/while/body/eval_jaxpr/ppermute | solution.py:19
  145.3 2.3 bitcast_dynamic-update-slice_fusion.6
  147.6 6.2 %fusion.29 = (bf16[128,2048]{1,0:T(8,128)(2,1)}, f32[128,2048]{1,0:T(8,128)}) fusion(bf16[128,2048]{1,0:T(8,128)(2,1)S(1)} %get-tuple-element.333, bf16[2048,2048]{1,0:T(8,128)(2,1)} %get-tuple-element.380), kind=kOutput, calls=%fused_computation.7.clone.1 | convolution fusion | flops 1076625408 | bytes 10485760 | tf_op jit(solution)/shard_map/while/body/eval_jaxpr/dot_general | solution.py:428
  158.1 6.5 %collective-permute-done = bf16[128,2048]{1,0:T(8,128)(2,1)} collective-permute-done((bf16[128,2048]{1,0:T(8,128)(2,1)}, bf16[128,2048]{1,0:T(8,128)(2,1)}, u32[]{:S(2)}, u32[]{:S(2)}) %collective-permute-start) | collective-permute-done | bytes 524320 | tf_op jit(solution)/shard_map/while/body/eval_jaxpr/ppermute | solution.py:19
  166.2 145.3 %while.30 = (s32[]{:T(128)}, bf16[128,2048]{1,0:T(8,128)(2,1)S(1)}, bf16[4,128,2048]{2,1,0:T(8,128)(2,1)}, s32[7]{0:T(128)S(1)}, s32[]{:T(128)}, /*index=5*/pred...) while((s32[]{:T(128)}, bf16[128,2048]{1,0:T(8,128)(2,1)S(1)}, ...), condition=%wide.region_4.5_spmd, body=%wide.region_3.4_spmd.sunk | while | flops 1086849024 | bytes 19402484 | solution.py:467
  167.5 7.9 %fusion.32 = bf16[128,2048]{1,0:T(8,128)(2,1)} fusion(bf16[2048,2048]{1,0:T(8,128)(2,1)} %get-tuple-element.419, bf16[128,2048]{1,0:T(8,128)(2,1)S(1)} %get-tuple-element.399, bf16[4,128,2048]{2,1,0:T(8,128)(2,1)} %get-tuple-element.417, s32[]{:T(128)S(6)} %min.13, pred[]{:T(512)} %get-tuple-element.416, pred[]{:T(512)S(6)} %and.22, ...), kind=kOutput, calls=%fused_computation.16.clone.1 | convolution fusion | flops 1080819712 | bytes 12061696 | tf_op jit(solution)/shard_map/while/body/eval_jaxpr/dot_general | solution.py:459
  178.4 3.0 bitcast_dynamic-update-slice_fusion.8
  181.4 2.9 collective-permute-done.1
  186.6 7.9 %fusion.32 = bf16[128,2048]{1,0:T(8,128)(2,1)} fusion(bf16[2048,2048]{1,0:T(8,128)(2,1)} %get-tuple-element.419, bf16[128,2048]{1,0:T(8,128)(2,1)S(1)} %get-tuple-element.399, bf16[4,128,2048]{2,1,0:T(8,128)(2,1)} %get-tuple-element.417, s32[]{:T(128)S(6)} %min.13, pred[]{:T(512)} %get-tuple-element.416, pred[]{:T(512)S(6)} %and.22, ...), kind=kOutput, calls=%fused_computation.16.clone.1 | convolution fusion | flops 1080819712 | bytes 12061696 | tf_op jit(solution)/shard_map/while/body/eval_jaxpr/dot_general | solution.py:459
  194.5 3.8 collective-permute-start.1
  199.4 3.0 bitcast_dynamic-update-slice_fusion.8
  202.5 2.9 collective-permute-done.1
  207.7 7.9 %fusion.32 = bf16[128,2048]{1,0:T(8,128)(2,1)} fusion(bf16[2048,2048]{1,0:T(8,128)(2,1)} %get-tuple-element.419, bf16[128,2048]{1,0:T(8,128)(2,1)S(1)} %get-tuple-element.399, bf16[4,128,2048]{2,1,0:T(8,128)(2,1)} %get-tuple-element.417, s32[]{:T(128)S(6)} %min.13, pred[]{:T(512)} %get-tuple-element.416, pred[]{:T(512)S(6)} %and.22, ...), kind=kOutput, calls=%fused_computation.16.clone.1 | convolution fusion | flops 1080819712 | bytes 12061696 | tf_op jit(solution)/shard_map/while/body/eval_jaxpr/dot_general | solution.py:459
  215.6 3.8 collective-permute-start.1
  220.5 3.0 bitcast_dynamic-update-slice_fusion.8
  223.5 2.9 collective-permute-done.1
  228.7 7.9 %fusion.32 = bf16[128,2048]{1,0:T(8,128)(2,1)} fusion(bf16[2048,2048]{1,0:T(8,128)(2,1)} %get-tuple-element.419, bf16[128,2048]{1,0:T(8,128)(2,1)S(1)} %get-tuple-element.399, bf16[4,128,2048]{2,1,0:T(8,128)(2,1)} %get-tuple-element.417, s32[]{:T(128)S(6)} %min.13, pred[]{:T(512)} %get-tuple-element.416, pred[]{:T(512)S(6)} %and.22, ...), kind=kOutput, calls=%fused_computation.16.clone.1 | convolution fusion | flops 1080819712 | bytes 12061696 | tf_op jit(solution)/shard_map/while/body/eval_jaxpr/dot_general | solution.py:459
  236.6 3.8 collective-permute-start.1
  241.5 3.0 bitcast_dynamic-update-slice_fusion.8
  244.5 2.9 collective-permute-done.1
  249.7 7.9 %fusion.32 = bf16[128,2048]{1,0:T(8,128)(2,1)} fusion(bf16[2048,2048]{1,0:T(8,128)(2,1)} %get-tuple-element.419, bf16[128,2048]{1,0:T(8,128)(2,1)S(1)} %get-tuple-element.399, bf16[4,128,2048]{2,1,0:T(8,128)(2,1)} %get-tuple-element.417, s32[]{:T(128)S(6)} %min.13, pred[]{:T(512)} %get-tuple-element.416, pred[]{:T(512)S(6)} %and.22, ...), kind=kOutput, calls=%fused_computation.16.clone.1 | convolution fusion | flops 1080819712 | bytes 12061696 | tf_op jit(solution)/shard_map/while/body/eval_jaxpr/dot_general | solution.py:459
  257.6 3.8 collective-permute-start.1
  262.5 3.0 bitcast_dynamic-update-slice_fusion.8
  265.5 2.9 collective-permute-done.1
  270.7 7.9 %fusion.32 = bf16[128,2048]{1,0:T(8,128)(2,1)} fusion(bf16[2048,2048]{1,0:T(8,128)(2,1)} %get-tuple-element.419, bf16[128,2048]{1,0:T(8,128)(2,1)S(1)} %get-tuple-element.399, bf16[4,128,2048]{2,1,0:T(8,128)(2,1)} %get-tuple-element.417, s32[]{:T(128)S(6)} %min.13, pred[]{:T(512)} %get-tuple-element.416, pred[]{:T(512)S(6)} %and.22, ...), kind=kOutput, calls=%fused_computation.16.clone.1 | convolution fusion | flops 1080819712 | bytes 12061696 | tf_op jit(solution)/shard_map/while/body/eval_jaxpr/dot_general | solution.py:459
  278.6 3.8 collective-permute-start.1
  283.5 3.0 bitcast_dynamic-update-slice_fusion.8
  286.6 2.9 collective-permute-done.1
  291.8 7.9 %fusion.32 = bf16[128,2048]{1,0:T(8,128)(2,1)} fusion(bf16[2048,2048]{1,0:T(8,128)(2,1)} %get-tuple-element.419, bf16[128,2048]{1,0:T(8,128)(2,1)S(1)} %get-tuple-element.399, bf16[4,128,2048]{2,1,0:T(8,128)(2,1)} %get-tuple-element.417, s32[]{:T(128)S(6)} %min.13, pred[]{:T(512)} %get-tuple-element.416, pred[]{:T(512)S(6)} %and.22, ...), kind=kOutput, calls=%fused_computation.16.clone.1 | convolution fusion | flops 1080819712 | bytes 12061696 | tf_op jit(solution)/shard_map/while/body/eval_jaxpr/dot_general | solution.py:459
  299.7 3.8 collective-permute-start.1
  304.6 3.0 bitcast_dynamic-update-slice_fusion.8
  307.6 2.9 collective-permute-done.1
  312.1 109.7 %dp_part.1 = (bf16[4,4,4,2,64,512]{5,4,3,2,1,0:T(8,128)(2,1)}, f32[64,64]{1,0:T(8,128)}) custom-call(s32[32]{0:T(128)} %select_reduce_fusion.blocks_ref, bf16[512,2048]{1,0:T(8,128)(2,1)} %bitcast.96, bf16[512,2048]{1,0:T(8,128)(2,1)} %bitcast.97, f32[64,64]{1,0:T(8,128)} %bitcast.99), custom_call_target="tpu_custom_call" | custom-call | tf_op jit(solution)/shard_map/dp_part/pallas_call | solution.py:324
  421.9 3.4 copy-done.1
  425.3 8.9 %restore.1 = bf16[32,64,2048]{2,1,0:T(8,128)(2,1)} custom-call(s32[32]{0:T(128)S(1)} %copy-done.2, bf16[4,4,4,2,64,512]{5,4,3,2,1,0:T(8,128)(2,1)S(1)} %copy-done.1), custom_call_target="tpu_custom_call" | custom-call | tf_op jit(solution)/shard_map/restore/pallas_call | solution.py:391
  (69 shorter events, 58.5 us)
Async XLA Ops:
  0.6 1.6 copy-start
  2.2 2.0 copy-start.4
  23.4 10.8 %collective-permute-start = (bf16[128,2048]{1,0:T(8,128)(2,1)}, bf16[128,2048]{1,0:T(8,128)(2,1)}, u32[]{:S(2)}, u32[]{:S(2)}) collective-permute-start(bf16[128,2048]{1,0:T(8,128)(2,1)} %get-tuple-element.334), channel_id=1, source_target_pairs={{0,32},{32,64},{64,96},{1,33},{33,65},{65,97},{2,34},{34,66},{66,9... | collective-permute-start | bytes 1572872 | tf_op jit(solution)/shard_map/while/body/eval_jaxpr/ppermute | solution.py:19
  45.1 10.8 %collective-permute-start = (bf16[128,2048]{1,0:T(8,128)(2,1)}, bf16[128,2048]{1,0:T(8,128)(2,1)}, u32[]{:S(2)}, u32[]{:S(2)}) collective-permute-start(bf16[128,2048]{1,0:T(8,128)(2,1)} %get-tuple-element.334), channel_id=1, source_target_pairs={{0,32},{32,64},{64,96},{1,33},{33,65},{65,97},{2,34},{34,66},{66,9... | collective-permute-start | bytes 1572872 | tf_op jit(solution)/shard_map/while/body/eval_jaxpr/ppermute | solution.py:19
  66.9 10.8 %collective-permute-start = (bf16[128,2048]{1,0:T(8,128)(2,1)}, bf16[128,2048]{1,0:T(8,128)(2,1)}, u32[]{:S(2)}, u32[]{:S(2)}) collective-permute-start(bf16[128,2048]{1,0:T(8,128)(2,1)} %get-tuple-element.334), channel_id=1, source_target_pairs={{0,32},{32,64},{64,96},{1,33},{33,65},{65,97},{2,34},{34,66},{66,9... | collective-permute-start | bytes 1572872 | tf_op jit(solution)/shard_map/while/body/eval_jaxpr/ppermute | solution.py:19
  88.6 10.8 %collective-permute-start = (bf16[128,2048]{1,0:T(8,128)(2,1)}, bf16[128,2048]{1,0:T(8,128)(2,1)}, u32[]{:S(2)}, u32[]{:S(2)}) collective-permute-start(bf16[128,2048]{1,0:T(8,128)(2,1)} %get-tuple-element.334), channel_id=1, source_target_pairs={{0,32},{32,64},{64,96},{1,33},{33,65},{65,97},{2,34},{34,66},{66,9... | collective-permute-start | bytes 1572872 | tf_op jit(solution)/shard_map/while/body/eval_jaxpr/ppermute | solution.py:19
  110.3 10.8 %collective-permute-start = (bf16[128,2048]{1,0:T(8,128)(2,1)}, bf16[128,2048]{1,0:T(8,128)(2,1)}, u32[]{:S(2)}, u32[]{:S(2)}) collective-permute-start(bf16[128,2048]{1,0:T(8,128)(2,1)} %get-tuple-element.334), channel_id=1, source_target_pairs={{0,32},{32,64},{64,96},{1,33},{33,65},{65,97},{2,34},{34,66},{66,9... | collective-permute-start | bytes 1572872 | tf_op jit(solution)/shard_map/while/body/eval_jaxpr/ppermute | solution.py:19
  132.0 10.8 %collective-permute-start = (bf16[128,2048]{1,0:T(8,128)(2,1)}, bf16[128,2048]{1,0:T(8,128)(2,1)}, u32[]{:S(2)}, u32[]{:S(2)}) collective-permute-start(bf16[128,2048]{1,0:T(8,128)(2,1)} %get-tuple-element.334), channel_id=1, source_target_pairs={{0,32},{32,64},{64,96},{1,33},{33,65},{65,97},{2,34},{34,66},{66,9... | collective-permute-start | bytes 1572872 | tf_op jit(solution)/shard_map/while/body/eval_jaxpr/ppermute | solution.py:19
  153.7 10.8 %collective-permute-start = (bf16[128,2048]{1,0:T(8,128)(2,1)}, bf16[128,2048]{1,0:T(8,128)(2,1)}, u32[]{:S(2)}, u32[]{:S(2)}) collective-permute-start(bf16[128,2048]{1,0:T(8,128)(2,1)} %get-tuple-element.334), channel_id=1, source_target_pairs={{0,32},{32,64},{64,96},{1,33},{33,65},{65,97},{2,34},{34,66},{66,9... | collective-permute-start | bytes 1572872 | tf_op jit(solution)/shard_map/while/body/eval_jaxpr/ppermute | solution.py:19
  166.2 145.3 %copy-start.2 = (s32[32]{0:T(128)S(1)}, s32[32]{0:T(128)}, u32[]{:S(2)}) copy-start(s32[32]{0:T(128)} %owner_ref.1) | copy-start | bytes 388
  175.4 8.9 %collective-permute-start.1 = (bf16[128,2048]{1,0:T(8,128)(2,1)}, bf16[128,2048]{1,0:T(8,128)(2,1)}, u32[]{:S(2)}, u32[]{:S(2)}) collective-permute-start(bf16[128,2048]{1,0:T(8,128)(2,1)} %fusion.32), channel_id=1, source_target_pairs={{32,0},{64,32},{96,64},{33,1},{65,33},{97,65},{34,2},{66,34},{98,6... | collective-permute-start | bytes 1572872 | tf_op jit(solution)/shard_map/while/body/eval_jaxpr/ppermute | solution.py:19
  194.5 10.8 %collective-permute-start.1 = (bf16[128,2048]{1,0:T(8,128)(2,1)}, bf16[128,2048]{1,0:T(8,128)(2,1)}, u32[]{:S(2)}, u32[]{:S(2)}) collective-permute-start(bf16[128,2048]{1,0:T(8,128)(2,1)} %fusion.32), channel_id=1, source_target_pairs={{32,0},{64,32},{96,64},{33,1},{65,33},{97,65},{34,2},{66,34},{98,6... | collective-permute-start | bytes 1572872 | tf_op jit(solution)/shard_map/while/body/eval_jaxpr/ppermute | solution.py:19
  215.6 10.8 %collective-permute-start.1 = (bf16[128,2048]{1,0:T(8,128)(2,1)}, bf16[128,2048]{1,0:T(8,128)(2,1)}, u32[]{:S(2)}, u32[]{:S(2)}) collective-permute-start(bf16[128,2048]{1,0:T(8,128)(2,1)} %fusion.32), channel_id=1, source_target_pairs={{32,0},{64,32},{96,64},{33,1},{65,33},{97,65},{34,2},{66,34},{98,6... | collective-permute-start | bytes 1572872 | tf_op jit(solution)/shard_map/while/body/eval_jaxpr/ppermute | solution.py:19
  236.6 10.8 %collective-permute-start.1 = (bf16[128,2048]{1,0:T(8,128)(2,1)}, bf16[128,2048]{1,0:T(8,128)(2,1)}, u32[]{:S(2)}, u32[]{:S(2)}) collective-permute-start(bf16[128,2048]{1,0:T(8,128)(2,1)} %fusion.32), channel_id=1, source_target_pairs={{32,0},{64,32},{96,64},{33,1},{65,33},{97,65},{34,2},{66,34},{98,6... | collective-permute-start | bytes 1572872 | tf_op jit(solution)/shard_map/while/body/eval_jaxpr/ppermute | solution.py:19
  257.6 10.8 %collective-permute-start.1 = (bf16[128,2048]{1,0:T(8,128)(2,1)}, bf16[128,2048]{1,0:T(8,128)(2,1)}, u32[]{:S(2)}, u32[]{:S(2)}) collective-permute-start(bf16[128,2048]{1,0:T(8,128)(2,1)} %fusion.32), channel_id=1, source_target_pairs={{32,0},{64,32},{96,64},{33,1},{65,33},{97,65},{34,2},{66,34},{98,6... | collective-permute-start | bytes 1572872 | tf_op jit(solution)/shard_map/while/body/eval_jaxpr/ppermute | solution.py:19
  278.6 10.8 %collective-permute-start.1 = (bf16[128,2048]{1,0:T(8,128)(2,1)}, bf16[128,2048]{1,0:T(8,128)(2,1)}, u32[]{:S(2)}, u32[]{:S(2)}) collective-permute-start(bf16[128,2048]{1,0:T(8,128)(2,1)} %fusion.32), channel_id=1, source_target_pairs={{32,0},{64,32},{96,64},{33,1},{65,33},{97,65},{34,2},{66,34},{98,6... | collective-permute-start | bytes 1572872 | tf_op jit(solution)/shard_map/while/body/eval_jaxpr/ppermute | solution.py:19
  299.7 10.8 %collective-permute-start.1 = (bf16[128,2048]{1,0:T(8,128)(2,1)}, bf16[128,2048]{1,0:T(8,128)(2,1)}, u32[]{:S(2)}, u32[]{:S(2)}) collective-permute-start(bf16[128,2048]{1,0:T(8,128)(2,1)} %fusion.32), channel_id=1, source_target_pairs={{32,0},{64,32},{96,64},{33,1},{65,33},{97,65},{34,2},{66,34},{98,6... | collective-permute-start | bytes 1572872 | tf_op jit(solution)/shard_map/while/body/eval_jaxpr/ppermute | solution.py:19
  421.9 3.4 copy-start.1
  425.3 8.9 %copy-start.3 = (f32[64,64]{1,0:T(8,128)S(1)}, f32[64,64]{1,0:T(8,128)}, u32[]{:S(2)}) copy-start(f32[64,64]{1,0:T(8,128)} %get-tuple-element.187) | copy-start | bytes 49156

commit v2 on v1

--- a/solution.py
+++ b/solution.py
@@ -8,27 +8,225 @@
 from jax.sharding import PartitionSpec as P
 
 MESH = pl.DeviceIdType.MESH
-
 coef = 0.7978845608028654
 cubic = 0.044715
 
 
-def passed_along(block, axis, distance):
-    devices = range(lax.axis_size(axis))
-    route = [(i - distance, i) for i in devices if i - distance in devices]
-    return lax.ppermute(block, axis, route)
-
-
-def gelu_value(z):
-    tanh_part = jnp.tanh(coef * (z + cubic * z * z * z))
-    return 0.5 * z * (1.0 + tanh_part)
-
-
-def gelu_slope(z):
-    tanh_part = jnp.tanh(coef * (z + cubic * z * z * z))
-    return 0.5 * (1.0 + tanh_part) + 0.5 * z * (1.0 - tanh_part * tanh_part) * coef * (
-        1.0 + 3.0 * cubic * z * z
-    )
+TILE = 512
+
+
+def relay_kernel(
+    order_ref,
+    inputs_ref,
+    cot_ref,
+    weight_ref,
+    acts_ref,
+    slopes_ref,
+    w,
+    feed,
+    held,
+    slope,
+    onward,
+    grads,
+    dz,
+    back,
+    w_sem,
+    in_sem,
+    out_sem,
+    f_send,
+    f_recv,
+    b_send,
+    b_recv,
+):
+    s = lax.axis_index("section")
+    n_micro, rows, width = held.shape
+    n_tiles = width // TILE
+    last = 3
+
+    barrier = pltpu.get_barrier_semaphore()
+    for dev in ((s + 1) % 4, (s + 3) % 4):
+        pl.semaphore_signal(barrier, inc=1, device_id={"section": dev}, device_id_type=MESH)
+
+    def columns(t):
+        return slice(t * TILE, (t + 1) * TILE)
+
+    def w_copy(t):
+        return pltpu.make_async_copy(weight_ref.at[0, :, columns(t)], w.at[:, columns(t)], w_sem.at[t])
+
+    feed_copy = pltpu.make_async_copy(inputs_ref, feed, in_sem)
+    cot_copy = pltpu.make_async_copy(cot_ref, grads, in_sem)
+
+    @pl.when(s == 0)
+    def _():
+        feed_copy.start()
+
+    for t in range(n_tiles):
+        w_copy(t).start()
+
+    @pl.when(s == last)
+    def _():
+        cot_copy.start()
+
+    pl.semaphore_wait(barrier, 2)
+
+    @pl.when(s == 0)
+    def _():
+        feed_copy.wait()
+
+    @pl.when(s == last)
+    def _():
+        cot_copy.wait()
+
+    def forward_copy(k, t):
+        return pltpu.make_async_remote_copy(
+            src_ref=onward.at[k, :, columns(t)],
+            dst_ref=held.at[k, :, columns(t)],
+            send_sem=f_send.at[k, t],
+            recv_sem=f_recv.at[k, t],
+            device_id={"section": (s + 1) % 4},
+            device_id_type=MESH,
+        )
+
+    def backward_copy(k, t):
+        return pltpu.make_async_remote_copy(
+            src_ref=back.at[k, :, columns(t)],
+            dst_ref=grads.at[k, :, columns(t)],
+            send_sem=b_send.at[k, t],
+            recv_sem=b_recv.at[k, t],
+            device_id={"section": (s + 3) % 4},
+            device_id_type=MESH,
+        )
+
+    def acts_copy(k):
+        return pltpu.make_async_copy(held.at[k], acts_ref.at[k], out_sem.at[0, k])
+
+    def slopes_copy(k):
+        return pltpu.make_async_copy(dz.at[k], slopes_ref.at[k], out_sem.at[1, k])
+
+    def forward(k):
+        @pl.when(s == 0)
+        def _():
+            held[k] = feed[order_ref[k]]
+
+        @pl.when(s > 0)
+        def _():
+            for t in range(n_tiles):
+                forward_copy(k, t).wait_recv()
+
+        acts_copy(k).start()
+        for t in range(n_tiles):
+
+            @pl.when(k == 0)
+            def _():
+                w_copy(t).wait()
+
+            z = jnp.dot(held[k], w[:, columns(t)], preferred_element_type=jnp.float32)
+            square = z * z
+            tanh_part = jnp.tanh(coef * (z + cubic * square * z))
+            half = 0.5 * (1.0 + tanh_part)
+            slope[k, :, columns(t)] = half + 0.5 * z * (1.0 - tanh_part * tanh_part) * coef * (
+                1.0 + 3.0 * cubic * square
+            )
+
+            @pl.when(s < last)
+            def _():
+                before = held[k, :, columns(t)].astype(jnp.float32)
+                onward[k, :, columns(t)] = (before + z * half).astype(jnp.bfloat16)
+                forward_copy(k, t).start()
+
+    def backward(k):
+        @pl.when(s < last)
+        def _():
+            for t in range(n_tiles):
+                backward_copy(k, t).wait_recv()
+
+        for t in range(n_tiles):
+            g = grads[k, :, columns(t)].astype(jnp.float32)
+            dz[k, :, columns(t)] = (g * slope[k, :, columns(t)]).astype(jnp.bfloat16)
+        slopes_copy(k).start()
+
+        @pl.when(s > 0)
+        def _():
+            for t in range(n_tiles):
+                value = lax.dot_general(
+                    dz[k],
+                    w[columns(t), :],
+                    (((1,), (1,)), ((), ())),
+                    preferred_element_type=jnp.float32,
+                )
+                g = grads[k, :, columns(t)].astype(jnp.float32)
+                back[k, :, columns(t)] = (g + value).astype(jnp.bfloat16)
+                backward_copy(k, t).start()
+
+    def step(k, carry):
+        @pl.when(k < n_micro)
+        def _():
+            forward(k)
+
+        b = k - (last - s)
+
+        @pl.when((b >= 0) & (b < n_micro))
+        def _():
+            backward(b)
+
+        return carry
+
+    lax.fori_loop(0, n_micro + last, step, 0)
+
+    def drain(k, carry):
+        acts_copy(k).wait()
+        slopes_copy(k).wait()
+
+        @pl.when(s < last)
+        def _():
+            for t in range(n_tiles):
+                forward_copy(k, t).wait_send()
+
+        @pl.when(s > 0)
+        def _():
+            for t in range(n_tiles):
+                backward_copy(k, t).wait_send()
+
+        return carry
+
+    lax.fori_loop(0, n_micro, drain, 0)
+
+
+def relay(inputs, cotangent, weights, order):
+    n_micro, rows, width = inputs.shape
+    n_tiles = width // TILE
+    bf = jnp.bfloat16
+    hbm = pl.BlockSpec(memory_space=pl.ANY)
+    block = pltpu.VMEM((n_micro, rows, width), bf)
+    dma = pltpu.SemaphoreType.DMA
+    out = jax.ShapeDtypeStruct((n_micro, rows, width), bf)
+    return pl.pallas_call(
+        relay_kernel,
+        out_shape=(out, out),
+        in_specs=[pl.BlockSpec(memory_space=pltpu.SMEM), hbm, hbm, hbm],
+        out_specs=(hbm, hbm),
+        scratch_shapes=[
+            pltpu.VMEM((width, width), bf),
+            block,
+            block,
+            pltpu.VMEM((n_micro, rows, width), jnp.float32),
+            block,
+            block,
+            block,
+            block,
+            dma((n_tiles,)),
+            dma(()),
+            dma((2, n_micro)),
+            dma((n_micro, n_tiles)),
+            dma((n_micro, n_tiles)),
+            dma((n_micro, n_tiles)),
+            dma((n_micro, n_tiles)),
+        ],
+        compiler_params=pltpu.CompilerParams(
+            collective_id=0, has_side_effects=True, vmem_limit_bytes=60 * 1024 * 1024
+        ),
+        name="relay",
+    )(order, inputs, cotangent, weights)
 
 
 WIDE = 512
@@ -404,77 +602,17 @@
 
 
 def body(inputs, cotangent, weights, preconds, order, owner):
-    weight = weights[0]
-    sections = lax.axis_size("section")
-    place = lax.axis_index("section")
-    n_micro = inputs.shape[0]
-    tok_rows = inputs.shape[1]
     width = inputs.shape[2]
     n_group = owner.shape[0]
-    block = width // n_group
-    total_rows = n_micro * tok_rows * n_group
-    n_steps = n_micro + sections - 1
-    feed = jnp.take(inputs, order[0], axis=0)
-    saved_in = jnp.zeros((n_micro, tok_rows, width), jnp.bfloat16)
-    saved_pre = jnp.zeros((n_micro, tok_rows, width), jnp.float32)
-
-    def forward_step(carry, step):
-        incoming, kept_in, kept_pre = carry
-        slot = step - place
-        valid = (slot >= 0) & (slot < n_micro)
-        slot_c = jnp.clip(slot, 0, n_micro - 1)
-        first = lax.dynamic_index_in_dim(feed, slot_c, 0, keepdims=False)
-        current = jnp.where(place == 0, first, incoming)
-        pre = jnp.dot(current, weight, preferred_element_type=jnp.float32)
-        output = (current.astype(jnp.float32) + gelu_value(pre)).astype(jnp.bfloat16)
-        old_in = lax.dynamic_index_in_dim(kept_in, slot_c, 0, keepdims=False)
-        kept_in = lax.dynamic_update_index_in_dim(
-            kept_in, jnp.where(valid, current, old_in), slot_c, 0
-        )
-        old_pre = lax.dynamic_index_in_dim(kept_pre, slot_c, 0, keepdims=False)
-        kept_pre = lax.dynamic_update_index_in_dim(
-            kept_pre, jnp.where(valid, pre, old_pre), slot_c, 0
-        )
-        incoming = passed_along(output, "section", 1)
-        return ((incoming, kept_in, kept_pre), None)
-
-    start_rows = jnp.zeros((tok_rows, width), jnp.bfloat16)
-    (unused_rows, saved_in, saved_pre), _ = lax.scan(
-        forward_step, (start_rows, saved_in, saved_pre), jnp.arange(n_steps, dtype=jnp.int32)
-    )
-
-    def backward_step(carry, step):
-        incoming, kept = carry
-        slot = step - (sections - 1 - place)
-        valid = (slot >= 0) & (slot < n_micro)
-        slot_c = jnp.clip(slot, 0, n_micro - 1)
-        last = lax.dynamic_index_in_dim(cotangent, slot_c, 0, keepdims=False)
-        current = jnp.where(place == sections - 1, last, incoming)
-        current = jnp.where(valid, current, jnp.zeros_like(current))
-        acts = lax.dynamic_index_in_dim(saved_in, slot_c, 0, keepdims=False)
-        pre = lax.dynamic_index_in_dim(saved_pre, slot_c, 0, keepdims=False)
-        slopes = (current.astype(jnp.float32) * gelu_slope(pre)).astype(jnp.bfloat16)
-        old = lax.dynamic_index_in_dim(kept, slot_c, 0, keepdims=False)
-        kept = lax.dynamic_update_index_in_dim(kept, jnp.where(valid, slopes, old), slot_c, 0)
-        back = lax.dot_general(
-            slopes, weight, (((1,), (1,)), ((), ())), preferred_element_type=jnp.float32
-        )
-        sent = (current.astype(jnp.float32) + back).astype(jnp.bfloat16)
-        incoming = passed_along(sent, "section", -1)
-        return ((incoming, kept), None)
-
-    kept = jnp.zeros_like(saved_in)
-    (unused_back, kept), _ = lax.scan(
-        backward_step, (start_rows, kept), jnp.arange(n_steps, dtype=jnp.int32)
-    )
+    acts, slopes = relay(inputs, cotangent, weights, order[0])
     positions = jnp.arange(n_group, dtype=jnp.int32)
     matches = (owner[None, :] == positions[:, None]).astype(jnp.int32)
     blocks_of = jnp.sum(matches * positions[None, :], axis=1)
     gathered, gram = dp_part(
-        saved_in.reshape(-1, width), kept.reshape(-1, width), preconds[0, 0], blocks_of
+        acts.reshape(-1, width), slopes.reshape(-1, width), preconds[0, 0], blocks_of
     )
     result = restore(gathered, owner).reshape(1, width, width)
-    return (result, gram.reshape(1, 1, block, block))
+    return (result, gram.reshape(1, 1, *gram.shape))
 
 
 def solution(mesh):

time: 438 us -> 202 us (0.46)
  the two profiles are of different devices: /device:TPU:8 before, /device:TPU:0 now
where the time goes in v2:
time: 202 us
  Pallas kernels  196 us (97%)
  local copies, waits for them, and re-layouts  4 us (2%)
    pallas_call x1, Pallas kernels, dp_part(): pl.pallas_call(functools.partial(dp_kernel, KINDS, dp_order(n, LAG)), out...  115 us
    pallas_call x1, Pallas kernels, relay(): pl.pallas_call(relay_kernel, out_shape=(out, out), in_specs=[pl.BlockSpec...  71.4 us
    pallas_call x1, Pallas kernels, restore(): pl.pallas_call(restore_kernel, out_shape=jax.ShapeDtypeStruct((32, 64, n...  8.9 us

profile of v2, /device:TPU:0, one launch (start us, length us, event | category | flops | bytes accessed | tf_op | source)
XLA Modules:
  0.0 201.6 jit_solution(10454788364013205674)
XLA Ops:
  0.6 1.3 select_reduce_fusion.blocks_ref
  1.9 71.4 %relay.1 = (bf16[4,128,2048]{2,1,0:T(8,128)(2,1)}, bf16[4,128,2048]{2,1,0:T(8,128)(2,1)}) custom-call(s32[4]{0:T(128)} %bitcast.11, bf16[4,128,2048]{2,1,0:T(8,128)(2,1)} %inputs_ref.1, bf16[4,128,2048]{2,1,0:T(8,128)(2,1)} %cot_ref.1, bf16[1,2048,2048]{2,1,0:T(8,128)(2,1)} %weight_ref.1), custom_call_target="tpu_custom_call" | custom-call | tf_op jit(solution)/shard_map/relay/pallas_call | solution.py:203
  73.4 0.0 copy-start.1
  73.4 115.2 %dp_part.1 = (bf16[4,4,4,2,64,512]{5,4,3,2,1,0:T(8,128)(2,1)}, f32[64,64]{1,0:T(8,128)}) custom-call(s32[32]{0:T(128)} %select_reduce_fusion.blocks_ref, bf16[512,2048]{1,0:T(8,128)(2,1)} %bitcast.7, bf16[512,2048]{1,0:T(8,128)(2,1)} %bitcast.8, f32[64,64]{1,0:T(8,128)} %bitcast.9), custom_call_target="tpu_custom_call" | custom-call | tf_op jit(solution)/shard_map/dp_part/pallas_call | solution.py:522
  188.6 0.0 copy-done.1
  188.6 0.0 copy-start
  188.6 3.4 %copy-done = bf16[4,4,4,2,64,512]{5,4,3,2,1,0:T(8,128)(2,1)S(1)} copy-done((bf16[4,4,4,2,64,512]{5,4,3,2,1,0:T(8,128)(2,1)S(1)}, bf16[4,4,4,2,64,512]{5,4,3,2,1,0:T(8,128)(2,1)}, u32[]{:S(2)}) %copy-start) | copy-done | bytes 8388632
  192.0 0.0 copy-start.2
  192.0 8.9 %restore.1 = bf16[32,64,2048]{2,1,0:T(8,128)(2,1)} custom-call(s32[32]{0:T(128)S(1)} %copy-done.1, bf16[4,4,4,2,64,512]{5,4,3,2,1,0:T(8,128)(2,1)S(1)} %copy-done), custom_call_target="tpu_custom_call" | custom-call | tf_op jit(solution)/shard_map/restore/pallas_call | solution.py:589
  200.9 0.0 copy-done.2
  200.9 0.6 copy.9
Async XLA Ops:
  73.4 115.3 %copy-start.1 = (s32[32]{0:T(128)S(1)}, s32[32]{0:T(128)}, u32[]{:S(2)}) copy-start(s32[32]{0:T(128)} %owner_ref.1) | copy-start | bytes 388
  188.6 3.4 %copy-start = (bf16[4,4,4,2,64,512]{5,4,3,2,1,0:T(8,128)(2,1)S(1)}, bf16[4,4,4,2,64,512]{5,4,3,2,1,0:T(8,128)(2,1)}, u32[]{:S(2)}) copy-start(bf16[4,4,4,2,64,512]{5,4,3,2,1,0:T(8,128)(2,1)} %get-tuple-element.8.src_ref) | copy-start | bytes 25165828
  192.0 8.9 %copy-start.2 = (f32[64,64]{1,0:T(8,128)S(1)}, f32[64,64]{1,0:T(8,128)}, u32[]{:S(2)}) copy-start(f32[64,64]{1,0:T(8,128)} %get-tuple-element.9) | copy-start | bytes 49156

commit v3 on v0

v3 whole, which is shorter than its diff:
```python
import functools

import jax
import jax.numpy as jnp
from jax import lax
from jax.experimental import pallas as pl
from jax.experimental.pallas import tpu as pltpu
from jax.sharding import PartitionSpec as P

MESH = pl.DeviceIdType.MESH
coef = 0.7978845608028654
cubic = 0.044715


TILE = 512


def relay_kernel(
    order_ref,
    blocks_ref,
    inputs_ref,
    cot_ref,
    weight_ref,
    turned_ref,
    dz,
    g_part,
    w,
    feed,
    held,
    slope,
    onward,
    grads,
    back,
    total,
    flipped,
    w_sem,
    in_sem,
    f_send,
    f_recv,
    b_send,
    b_recv,
):
    s = lax.axis_index("section")
    n_micro, rows, width = held.shape
    n_tiles = width // TILE
    last = 3

    barrier = pltpu.get_barrier_semaphore()
    for dev in ((s + 1) % 4, (s + 3) % 4):
        pl.semaphore_signal(barrier, inc=1, device_id={"section": dev}, device_id_type=MESH)

    def tile(t):
        return slice(t * TILE, (t + 1) * TILE)

    def w_copy(t):
        return pltpu.make_async_copy(weight_ref.at[0, tile(t)], w.at[tile(t)], w_sem.at[t])

    feed_copy = pltpu.make_async_copy(inputs_ref, feed, in_sem)
    cot_copy = pltpu.make_async_copy(cot_ref, grads, in_sem)

    @pl.when(s == 0)
    def _():
        feed_copy.start()

    for t in range(n_tiles):
        w_copy(t).start()

    @pl.when(s == last)
    def _():
        cot_copy.start()

    g_part[...] = jnp.zeros(g_part.shape, g_part.dtype)
    pl.semaphore_wait(barrier, 2)

    @pl.when(s == 0)
    def _():
        feed_copy.wait()

    @pl.when(s == last)
    def _():
        cot_copy.wait()

    def forward_copy(k, t):
        return pltpu.make_async_remote_copy(
            src_ref=onward.at[k, :, tile(t)],
            dst_ref=held.at[k, :, tile(t)],
            send_sem=f_send.at[k, t],
            recv_sem=f_recv.at[k, t],
            device_id={"section": (s + 1) % 4},
            device_id_type=MESH,
        )

    def backward_copy(k, t):
        return pltpu.make_async_remote_copy(
            src_ref=back.at[k, :, tile(t)],
            dst_ref=grads.at[k, :, tile(t)],
            send_sem=b_send.at[k, t],
            recv_sem=b_recv.at[k, t],
            device_id={"section": (s + 3) % 4},
            device_id_type=MESH,
        )

    def forward(k):
        @pl.when(s == 0)
        def _():
            held[k] = feed[order_ref[k]]

        for j in range(n_tiles):

            @pl.when(s > 0)
            def _():
                forward_copy(k, j).wait_recv()

            @pl.when(k == 0)
            def _():
                w_copy(j).wait()

            for t in range(n_tiles):
                z = jnp.dot(held[k, :, tile(j)], w[tile(j), tile(t)], preferred_element_type=jnp.float32)
                if j > 0:
                    z = z + total[:, tile(t)]
                if j < n_tiles - 1:
                    total[:, tile(t)] = z
                    continue
                square = z * z
                tanh_part = jnp.tanh(coef * (z + cubic * square * z))
                half = 0.5 * (1.0 + tanh_part)

                @pl.when(s < last)
                def _():
                    before = held[k, :, tile(t)].astype(jnp.float32)
                    onward[k, :, tile(t)] = (before + z * half).astype(jnp.bfloat16)
                    forward_copy(k, t).start()

                slope[k, :, tile(t)] = half + 0.5 * z * (1.0 - tanh_part * tanh_part) * coef * (
                    1.0 + 3.0 * cubic * square
                )

    def backward(k):
        for j in range(n_tiles):

            @pl.when(s < last)
            def _():
                backward_copy(k, j).wait_recv()

            g = grads[k, :, tile(j)].astype(jnp.float32)
            piece = (g * slope[k, :, tile(j)]).astype(jnp.bfloat16)
            dz[k, :, tile(j)] = piece

            @pl.when(s > 0)
            def _():
                for t in range(n_tiles):
                    value = lax.dot_general(
                        dz[k, :, tile(j)],
                        w[tile(t), tile(j)],
                        (((1,), (1,)), ((), ())),
                        preferred_element_type=jnp.float32,
                    )
                    if j > 0:
                        value = value + total[:, tile(t)]
                    if j < n_tiles - 1:
                        total[:, tile(t)] = value
                        continue
                    g = grads[k, :, tile(t)].astype(jnp.float32)
                    back[k, :, tile(t)] = (g + value).astype(jnp.bfloat16)
                    backward_copy(k, t).start()

    def turn(k):
        for part in range(8):
            block = held[k, :, part * 256 : (part + 1) * 256].T
            flipped[part * 4 : (part + 1) * 4] = block.reshape(4, 64, rows)

        lanes = pl.ds(pl.multiple_of(k * rows, rows), rows)

        def move(p, carry):
            turned_ref[p // 8, (p // 2) % 4, p % 2, :, lanes] = flipped[blocks_ref[p]]
            return carry

        lax.fori_loop(0, 32, move, 0)

    def squares():
        for z in range(4):
            for pair in range(2):
                left = turned_ref[z, pair * 2 : pair * 2 + 2].reshape(256, n_micro * rows)
                square = lax.dot_general(left, left, (((1,), (1,)), ((), ())), preferred_element_type=jnp.float32)
                for i in range(4):
                    lanes = slice(i * 64, (i + 1) * 64)
                    value = square[lanes, lanes].astype(jnp.bfloat16)
                    g_part[pair * 2 + i // 2, z // 2, z % 2, i % 2, :, 0:64] = value

    def step(k, carry):
        @pl.when(k < n_micro)
        def _():
            forward(k)

        b = k - (last - s)

        @pl.when((b >= 0) & (b < n_micro))
        def _():
            backward(b)

        @pl.when(k < n_micro)
        def _():
            turn(k)

        @pl.when(k == n_micro - 1)
        def _():
            squares()

        return carry

    lax.fori_loop(0, n_micro + last, step, 0)

    def drain(k, carry):
        @pl.when(s < last)
        def _():
            for t in range(n_tiles):
                forward_copy(k, t).wait_send()

        @pl.when(s > 0)
        def _():
            for t in range(n_tiles):
                backward_copy(k, t).wait_send()

        return carry

    lax.fori_loop(0, n_micro, drain, 0)


def relay(inputs, cotangent, weights, order, blocks_of):
    n_micro, rows, width = inputs.shape
    n_tiles = width // TILE
    bf = jnp.bfloat16
    hbm, vmem = pl.BlockSpec(memory_space=pl.ANY), pl.BlockSpec(memory_space=pltpu.VMEM)
    smem = pl.BlockSpec(memory_space=pltpu.SMEM)
    block = pltpu.VMEM((n_micro, rows, width), bf)
    dma = pltpu.SemaphoreType.DMA
    return pl.pallas_call(
        relay_kernel,
        out_shape=(
            pltpu.VMEM((4, 4, 2, 64, n_micro * rows), bf),
            block,
            pltpu.VMEM(ring_shape(GRAM[0], GRAM[1]), bf),
        ),
        in_specs=[smem, smem, hbm, hbm, hbm],
        out_specs=(vmem, vmem, vmem),
        scratch_shapes=[
            pltpu.VMEM((width, width), bf),
            block,
            block,
            pltpu.VMEM((n_micro, rows, width), jnp.float32),
            block,
            block,
            block,
            pltpu.VMEM((rows, width), jnp.float32),
            pltpu.VMEM((32, 64, rows), bf),
            dma((n_tiles,)),
            dma(()),
            dma((n_micro, n_tiles)),
            dma((n_micro, n_tiles)),
            dma((n_micro, n_tiles)),
            dma((n_micro, n_tiles)),
        ],
        compiler_params=pltpu.CompilerParams(
            collective_id=0, has_side_effects=True, vmem_limit_bytes=48 * 1024 * 1024
        ),
        name="relay",
    )(order, blocks_of, inputs, cotangent, weights)


SIZES = {"x": 4, "z": 4, "y": 2}
CHUNKS = (("yxz", 256), ("yzx", 256), ("xzy", 256), ("zxy", 256), ("xzy", 256), ("zxy", 256), ("xzy", 256), ("zxy", 256))
GRAM = ("xzy", 128)
ORDER = (8, 7, 6, 0, 7, 6, 5, 2, 1, 5, 6, 2, 7, 0, 3, 2, 7, 6, 5, 0, 4, 3, 5, 7, 0, 1, 6, 7, 0, 4, 2, 8, 6, 1, 5, 0, 6, 7, 1, 0, 4, 3, 6, 7, 2, 1, 0, 5, 8, 3, 4, 7, 1, 8, 5, 4, 2, 3, 0, 1, 6, 2, 4, 7, 3, 8, 5, 1, 0, 4, 3, 8, 6, 2, 1, 3, 4, 2, 5, 4, 7, 3, 6, 1, 5, 2, 0, 4, 3, 2, 1, 5, 4, 3)


def ring_shape(dims, wide):
    if len(dims) == 1:
        return (4, 2, 32, wide)
    if dims[1] == "y":
        return (4, 2, *(SIZES[d] for d in dims[2:]), 64, wide)
    return (4, 2, 2, *(SIZES[d] for d in dims[2:]), 64, wide)


def phase_shapes(dims, wide):
    if dims[0] == "y":
        part = (2, *(SIZES[d] for d in dims[1:]), 64, wide)
        return part, part[1:]
    part = ring_shape(dims, wide)
    return part, (6, *part[2:])


def chunk_scratch(dims, wide):
    shapes = []
    for phase in range(3):
        shapes += phase_shapes(dims[phase:], wide)
    return [pltpu.VMEM(shape, jnp.bfloat16) for shape in shapes]


def dp_kernel(*refs):
    n = len(CHUNKS)
    h_p, dz_ref, pc_ref, squares_ref = refs[:4]
    fulls, gram_ref = refs[4 : 4 + n], refs[4 + n]
    send_sem, recv_sem = refs[5 + n : 7 + n]
    scratch = refs[7 + n :]
    scratch[6 * n][...] = squares_ref[...]

    me = lax.axis_index("dp")
    my_z, my_x, my_y = me // 8, (me // 2) % 4, me % 2

    def place(z, x, y):
        return z * 8 + x * 2 + y

    up_of, down_of, far_of = (lambda v: (v + 1) % 4), (lambda v: (v + 3) % 4), (lambda v: (v + 2) % 4)
    rings = {
        "x": (my_x, place(my_z, up_of(my_x), my_y), place(my_z, down_of(my_x), my_y)),
        "z": (my_z, place(up_of(my_z), my_x, my_y), place(down_of(my_z), my_x, my_y)),
    }
    mine = {"x": my_x, "z": my_z, "y": my_y}
    mate = place(my_z, my_x, 1 - my_y)

    barrier = pltpu.get_barrier_semaphore()
    for dev in (*rings["x"][1:], *rings["z"][1:], mate):
        pl.semaphore_signal(barrier, inc=1, device_id={"dp": dev}, device_id_type=MESH)

    rows = h_p.shape[-1]
    sent = []
    f32, bf16 = jnp.float32, jnp.bfloat16

    def left_rows(first, r, half_dim, half):
        if half_dim == "y":
            return (slice(None), r, half) if first == "x" else (r, slice(None), half)
        two = slice(2 * half, 2 * half + 2)
        return (two, r) if first == "x" else (r, two)

    def flow(slot, dims, wide, offset, bufs, full):
        cols = slice(offset, offset + wide)
        counter = [0]

        def remote(src, dst, dev):
            k = counter[0]
            counter[0] += 1
            copy = pltpu.make_async_remote_copy(
                src_ref=src,
                dst_ref=dst,
                send_sem=send_sem.at[slot, k],
                recv_sem=recv_sem.at[slot, k],
                device_id={"dp": dev},
                device_id_type=MESH,
            )
            copy.start()
            sent.append(copy)
            return copy

        def product(part, index, left):
            right = dz_ref[:, :, cols].reshape(rows, wide)
            value = jnp.dot(h_p[left].reshape(256, rows), right, preferred_element_type=f32)
            part[index] = value.astype(bf16).reshape(part.shape[len(index) :])

        def no_product(part, index, left):
            pass

        make = product if full is not None else no_product

        def store(part, ring_half, total):
            if ring_half is None:
                part[...] = total.astype(bf16).reshape(part.shape)
                return
            share = part.shape[0] // 2
            if share == 1:
                part[ring_half] = total.astype(bf16).reshape(part.shape[1:])
            else:
                where = slice(share * ring_half, share * ring_half + share)
                part[where] = total.astype(bf16).reshape(share, *part.shape[1:])

        total = None
        for phase in range(3):
            d = dims[phase]
            part, landed = bufs[2 * phase], bufs[2 * phase + 1]
            then = bufs[2 * phase + 2] if phase < 2 else None
            m = mine[d]
            if d == "y":
                other = 1 - my_y
                if phase == 0:
                    first = dims[1]
                    left = lambda r, y: (slice(None), r, y) if first == "x" else (r, slice(None), y)
                    copies = []
                    for r in range(4):
                        make(part, (other, r), left(r, other))
                        copies.append(remote(part.at[other, r], landed.at[r], mate))
                    for r in range(4):
                        make(part, (my_y, r), left(r, my_y))
                    yield
                    for r in range(4):
                        copies[r].wait_recv()
                        value = part[my_y, r].astype(f32) + landed[r].astype(f32)
                        then[r] = value.astype(bf16).reshape(then.shape[1:])
                else:
                    copy = remote(part.at[other], landed, mate)
                    yield
                    copy.wait_recv()
                    total = part[my_y].astype(f32) + landed[...].astype(f32)
                    if then is not None:
                        store(then, None, total)
                continue
            up, down, far = up_of(m), down_of(m), far_of(m)
            dev_up, dev_down = rings[d][1:]
            half_dim = dims[phase + 1] if phase < 2 else None
            fill = make if phase == 0 else no_product
            left = (lambda r, h: left_rows(d, r, half_dim, h)) if phase == 0 else (lambda r, h: None)
            fill(part, (far, 0), left(far, 0))
            mp = remote(part.at[far, 0], landed.at[0], dev_up)
            fill(part, (far, 1), left(far, 1))
            mm = remote(part.at[far, 1], landed.at[1], dev_down)
            fill(part, (up, 1), left(up, 1))
            dp = remote(part.at[up, 1], landed.at[2], dev_up)
            fill(part, (down, 0), left(down, 0))
            dm = remote(part.at[down, 0], landed.at[3], dev_down)
            fill(part, (up, 0), left(up, 0))
            fill(part, (down, 1), left(down, 1))
            yield
            mp.wait_recv()
            part[up, 0] = (part[up, 0].astype(f32) + landed[0].astype(f32)).astype(bf16)
            tp = remote(part.at[up, 0], landed.at[4], dev_up)
            mm.wait_recv()
            part[down, 1] = (part[down, 1].astype(f32) + landed[1].astype(f32)).astype(bf16)
            tm = remote(part.at[down, 1], landed.at[5], dev_down)
            fill(part, (m, 0), left(m, 0))
            fill(part, (m, 1), left(m, 1))
            yield
            halves = []
            for copy in (dp, dm, tp, tm):
                copy.wait_recv()
            for half, a, b in ((0, 3, 4), (1, 2, 5)):
                value = part[m, half].astype(f32) + landed[a].astype(f32) + landed[b].astype(f32)
                if then is not None:
                    store(then, half, value)
                halves.append(value)
            if then is None:
                total = jnp.concatenate(halves, axis=0)

        if full is None:
            gram_ref[...] = total[:, 0:64] * (1.0 / 16384.0)
            return
        done = jnp.dot(pc_ref[...], total, precision=lax.Precision.HIGHEST, preferred_element_type=f32)
        own = tuple(mine[d] for d in dims)
        full[own] = done.astype(bf16)
        for phase in (2, 1, 0):
            d = dims[phase]
            lead = own[:phase]
            slab = full.at[own[: phase + 1]]
            if d == "y":
                copy = remote(slab, slab, mate)
                yield
                copy.wait_recv()
                continue
            up, down = up_of(mine[d]), down_of(mine[d])
            dev_up, dev_down = rings[d][1:]

            def half_of(r, half):
                size = 64 if phase == 2 else SIZES[dims[phase + 1]]
                return full.at[(*lead, r, pl.ds(half * (size // 2), size // 2))]

            gp = remote(slab, slab, dev_up)
            gm = remote(slab, slab, dev_down)
            yield
            gp.wait_recv()
            block = half_of(down, 0)
            fp = remote(block, block, dev_up)
            gm.wait_recv()
            block = half_of(up, 1)
            fm = remote(block, block, dev_down)
            yield
            fp.wait_recv()
            fm.wait_recv()

    pl.semaphore_wait(barrier, 5)

    flows, offset = [], 0
    for slot, (dims, wide) in enumerate((*CHUNKS, GRAM)):
        bufs = scratch[6 * slot : 6 * slot + 6]
        flows.append(flow(slot, dims, wide, offset, bufs, fulls[slot] if slot < n else None))
        offset += wide
    for slot in ORDER:
        next(flows[slot], None)
    for copy in sent:
        copy.wait_send()


def gathered_shape(dims, wide):
    return (*(SIZES[d] for d in dims), 64, wide)


def dp_part(turned, slopes, precond, squares):
    n = len(CHUNKS)
    bf = jnp.bfloat16
    vmem = pl.BlockSpec(memory_space=pltpu.VMEM)
    dma = pltpu.SemaphoreType.DMA
    scratch = []
    for dims, wide in (*CHUNKS, GRAM):
        scratch += chunk_scratch(dims, wide)
    shapes = [gathered_shape(dims, wide) for dims, wide in CHUNKS]
    *gathered, gram = pl.pallas_call(
        dp_kernel,
        out_shape=(*(pltpu.VMEM(shape, bf) for shape in shapes), pltpu.VMEM((64, 64), jnp.float32)),
        in_specs=[vmem] * 4,
        out_specs=(*(vmem for _ in shapes), vmem),
        scratch_shapes=[dma((n + 1, 26)), dma((n + 1, 26)), *scratch],
        compiler_params=pltpu.CompilerParams(
            collective_id=1, has_side_effects=True, vmem_limit_bytes=44 * 1024 * 1024
        ),
        name="dp_part",
    )(turned, slopes, precond, squares)
    return gathered, gram


def restore_kernel(owner_ref, *refs):
    n = len(CHUNKS)
    sources, gram_ref, dst_ref, gram_out, sem, gram_sem = refs[:n], *refs[n:]
    gram_copy = pltpu.make_async_copy(gram_ref, gram_out, gram_sem)
    gram_copy.start()

    def puts(b):
        o = owner_ref[b]
        at = {"z": o // 8, "x": (o // 2) % 4, "y": o % 2}
        copies, offset = [], 0
        for c, (dims, wide) in enumerate(CHUNKS):
            src = sources[c].at[tuple(at[d] for d in dims)]
            copies.append(pltpu.make_async_copy(src, dst_ref.at[b, :, pl.ds(offset, wide)], sem.at[b, c]))
            offset += wide
        return copies

    def first(b, carry):
        for copy in puts(b):
            copy.start()
        return carry

    def second(b, carry):
        for copy in puts(b):
            copy.wait()
        return carry

    lax.fori_loop(0, 32, first, 0)
    lax.fori_loop(0, 32, second, 0)
    gram_copy.wait()


def restore(gathered, gram, owner):
    n = len(CHUNKS)
    width = sum(wide for _, wide in CHUNKS)
    hbm = pl.BlockSpec(memory_space=pl.ANY)
    return pl.pallas_call(
        restore_kernel,
        out_shape=(
            jax.ShapeDtypeStruct((32, 64, width), jnp.bfloat16),
            jax.ShapeDtypeStruct(gram.shape, gram.dtype),
        ),
        in_specs=[pl.BlockSpec(memory_space=pltpu.SMEM), *[pl.BlockSpec(memory_space=pltpu.VMEM)] * (n + 1)],
        out_specs=(hbm, hbm),
        scratch_shapes=[
            pltpu.SemaphoreType.DMA((32, n)),
            pltpu.SemaphoreType.DMA(()),
        ],
        compiler_params=pltpu.CompilerParams(vmem_limit_bytes=16 * 1024 * 1024),
        name="restore",
    )(owner, *gathered, gram)


def body(inputs, cotangent, weights, preconds, order, owner):
    width = inputs.shape[2]
    n_group = owner.shape[0]
    positions = jnp.arange(n_group, dtype=jnp.int32)
    matches = (owner[None, :] == positions[:, None]).astype(jnp.int32)
    blocks_of = jnp.sum(matches * positions[None, :], axis=1)
    turned, slopes, squares = relay(inputs, cotangent, weights, order[0], blocks_of)
    gathered, gram = dp_part(turned, slopes, preconds[0, 0], squares)
    result, gram = restore(gathered, gram, owner)
    result = result.reshape(1, width, width)
    return (result, gram.reshape(1, 1, *gram.shape))


def solution(mesh):
    placed = (
        P(None, "dp", None),
        P(None, "dp", None),
        P("section", None, None),
        P("section", "dp", None, None),
        P("dp", None),
        P(),
    )
    return jax.shard_map(
        body,
        mesh=mesh,
        in_specs=placed,
        out_specs=(P("section", None, None), P("section", "dp", None, None)),
        check_vma=False,
    )
```

time: 878 us -> 174 us (0.20)
  waiting for transfers between devices: 495 us -> 0 us
  matrix products: 185 us -> 0 us
  Pallas kernels: 0 us -> 169 us
  starting transfers between devices: 58.9 us -> 0 us
  other arithmetic: 56.3 us -> 0.77 us
  local copies, waits for them, and re-layouts: 56.4 us -> 3.32 us
  between operations: 13.9 us -> 0.83 us
  loops' own time: 9.9 us -> 0 us
    reduce_scatter x2 -> x0, waiting for transfers between devices: 395 us -> none  [the longest x1 213 us: body(): lax.psum_scatter(ordered, 'dp', scatter_dimension=0, tiled=True)]
    dot_general x23 -> x0, matrix products: 185 us -> none  [the longest x7 98.1 us: backward_step(): lax.dot_general(acts, slopes, (((0,), (0,)), ((), ())), preferred_element...]
    pallas_call x0 -> x3, Pallas kernels: none -> 169 us  [the longest x1 95.7 us: dp_part(): pl.pallas_call(dp_kernel, out_shape=(*(pltpu.VMEM(shape, bf) for shape in...]
    all_gather x1 -> x0, waiting for transfers between devices: 100 us -> none  [body(): lax.all_gather(rows_mine.astype(jnp.bfloat16)[None], 'dp', axis=0, tiled=...]
    ppermute x14 -> x0, starting transfers between devices: 58.6 us -> none  [passed_along(): return lax.ppermute(block, axis, route)]
    dynamic_slice x28 -> x0, local copies, waits for them, and re-layouts: 25.6 us -> none  [the longest x7 9.26 us: forward_step(): old_pre = lax.dynamic_index_in_dim(kept_pre, slot_c, 0, keepdims=False)]
    dynamic_update_slice x14 -> x0, other arithmetic: 22.9 us -> none  [the longest x7 15.1 us: forward_step(): lax.dynamic_update_index_in_dim(kept_in, jnp.where(valid, current, old_in...]
    select_n x7 -> x0, other arithmetic: 20 us -> none  [the longest x2 8.23 us: body(): ordered = jnp.take(parts, blocks_of, axis=0)]
  transfers between devices with their start and end apart: 17 -> 0, of which waited for: 3 -> 0; matrix products, arithmetic and copies ran while one was open for 14% -> 0% of each run, Pallas kernels for 0% -> 0%
where the time goes in v3:
time: 174 us
  Pallas kernels  169 us (97%)
  local copies, waits for them, and re-layouts  3.32 us (2%)
    pallas_call x1, Pallas kernels, dp_part(): pl.pallas_call(dp_kernel, out_shape=(*(pltpu.VMEM(shape, bf) for shape in...  95.7 us
    pallas_call x1, Pallas kernels, relay(): pl.pallas_call(relay_kernel, out_shape=(pltpu.VMEM((4, 4, 2, 64, n_micro...  67.6 us
    pallas_call x1, Pallas kernels, restore(): pl.pallas_call(restore_kernel, out_shape=(jax.ShapeDtypeStruct((32, 64, w...  6.03 us

profile of v3, /device:TPU:0, one launch (start us, length us, event | category | flops | bytes accessed | tf_op | source)
XLA Modules:
  0.0 174.2 jit_solution(809340661068242765)
XLA Ops:
  0.6 0.8 select_reduce_fusion.blocks_ref
  1.4 0.0 copy-start.3
  1.4 0.7 copy-done.3
  2.1 0.0 copy-start.2
  2.1 67.6 %relay.1 = (bf16[4,4,2,64,512]{4,3,2,1,0:T(8,128)(2,1)S(1)}, bf16[4,128,2048]{2,1,0:T(8,128)(2,1)S(1)}, bf16[4,2,2,2,64,128]{5,4,3,2,1,0:T(8,128)(2,1)S(1)}) custom-call(s32[4]{0:T(128)S(1)} %bitcast.5, s32[32]{0:T(128)S(1)} %select_reduce_fusion.blocks_ref, bf16[4,128,2048]{2,1,0:T(8,128)(2,1)} %inputs_ref.1, bf16[4,128,2048]{2,1,0:T(8,128)(2,1)} %cot_ref.1, ...), custom_call_target="tpu_custom_call" | custom-call | tf_op jit(solution)/shard_map/relay/pallas_call | solution.py:238
  69.6 0.0 copy-start
  69.6 1.3 copy-done
  70.9 0.0 copy-start.1
  70.9 1.3 copy-done.1
  72.3 0.0 copy-done.2
  72.3 0.0 copy-start.4
  72.3 95.7 %dp_part.1 = (bf16[2,4,4,64,256]{4,3,2,1,0:T(8,128)(2,1)S(1)}, bf16[2,4,4,64,256]{4,3,2,1,0:T(8,128)(2,1)S(1)}, bf16[4,4,2,64,256]{4,3,2,1,0:T(8,128)(2,1)S(1)},...) custom-call(bf16[4,4,2,64,512]{4,3,2,1,0:T(8,128)(2,1)} %copy-done, ...), custom_call_target="tpu_custom_call" | custom-call | tf_op jit(solution)/shard_map/dp_part/pallas_call | solution.py:503
  168.0 0.0 copy-done.4
  168.0 6.0 %restore.1 = (bf16[32,64,2048]{2,1,0:T(8,128)(2,1)}, f32[64,64]{1,0:T(8,128)}) custom-call(s32[32]{0:T(128)S(1)} %copy-done.4, bf16[2,4,4,64,256]{4,3,2,1,0:T(8,128)(2,1)S(1)} %get-tuple-element.19.refs_0_, bf16[2,4,4,64,256]{4,3,2,1,0:T(8,128)(2,1)S(1)} %get-tuple-element.20.refs_1_, bf16[4,4,2,64,256]{4,3,2,1,0:T(8,128)(2,1)S(1)} %get-tuple-element.21.refs_2_, ...), custom_call_target="tpu_custom_call" | custom-call | tf_op jit(solution)/shard_map/restore/pallas_call | solution.py:552
Async XLA Ops:
  1.4 0.7 copy-start.3
  2.1 70.2 %copy-start.2 = (f32[1,1,64,64]{3,2,1,0:T(8,128)S(1)}, f32[1,1,64,64]{3,2,1,0:T(8,128)}, u32[]{:S(2)}) copy-start(f32[1,1,64,64]{3,2,1,0:T(8,128)} %param.9) | copy-start | bytes 49156
  69.6 1.3 copy-start
  70.9 1.3 copy-start.1
  72.3 95.7 %copy-start.4 = (s32[32]{0:T(128)S(1)}, s32[32]{0:T(128)}, u32[]{:S(2)}) copy-start(s32[32]{0:T(128)} %owner_ref.1) | copy-start | bytes 388

commit v4 on v3

--- a/solution.py
+++ b/solution.py
@@ -25,6 +25,7 @@
     dz,
     g_part,
     w,
+    w_t,
     feed,
     held,
     slope,
@@ -100,6 +101,16 @@
             device_id_type=MESH,
         )
 
+    def turn_weight():
+        def strip(r, carry):
+            at = pl.ds(pl.multiple_of(r * 256, 256), 256)
+            for c in range(width // 256):
+                cols = slice(c * 256, (c + 1) * 256)
+                w_t[cols, at] = w[at, cols].T
+            return carry
+
+        lax.fori_loop(0, width // 256, strip, 0)
+
     def forward(k):
         @pl.when(s == 0)
         def _():
@@ -111,7 +122,7 @@
             def _():
                 forward_copy(k, j).wait_recv()
 
-            @pl.when(k == 0)
+            @pl.when((k == 0) & (s < 2))
             def _():
                 w_copy(j).wait()
 
@@ -125,11 +136,11 @@
                 square = z * z
                 tanh_part = jnp.tanh(coef * (z + cubic * square * z))
                 half = 0.5 * (1.0 + tanh_part)
+                before = held[k, :, tile(t)].astype(jnp.float32)
+                onward[k, :, tile(t)] = (before + z * half).astype(jnp.bfloat16)
 
                 @pl.when(s < last)
                 def _():
-                    before = held[k, :, tile(t)].astype(jnp.float32)
-                    onward[k, :, tile(t)] = (before + z * half).astype(jnp.bfloat16)
                     forward_copy(k, t).start()
 
                 slope[k, :, tile(t)] = half + 0.5 * z * (1.0 - tanh_part * tanh_part) * coef * (
@@ -150,11 +161,8 @@
             @pl.when(s > 0)
             def _():
                 for t in range(n_tiles):
-                    value = lax.dot_general(
-                        dz[k, :, tile(j)],
-                        w[tile(t), tile(j)],
-                        (((1,), (1,)), ((), ())),
-                        preferred_element_type=jnp.float32,
+                    value = jnp.dot(
+                        dz[k, :, tile(j)], w_t[tile(j), tile(t)], preferred_element_type=jnp.float32
                     )
                     if j > 0:
                         value = value + total[:, tile(t)]
@@ -193,7 +201,11 @@
         def _():
             forward(k)
 
-        b = k - (last - s)
+        @pl.when((k == n_micro - 1) & (s == 1))
+        def _():
+            turn_weight()
+
+        b = k - jnp.where(s < 2, last, last - s)
 
         @pl.when((b >= 0) & (b < n_micro))
         def _():
@@ -208,6 +220,12 @@
             squares()
 
         return carry
+
+    @pl.when(s >= 2)
+    def _():
+        for t in range(n_tiles):
+            w_copy(t).wait()
+        turn_weight()
 
     lax.fori_loop(0, n_micro + last, step, 0)
 
@@ -246,6 +264,7 @@
         out_specs=(vmem, vmem, vmem),
         scratch_shapes=[
             pltpu.VMEM((width, width), bf),
+            pltpu.VMEM((width, width), bf),
             block,
             block,
             pltpu.VMEM((n_micro, rows, width), jnp.float32),
@@ -262,7 +281,7 @@
             dma((n_micro, n_tiles)),
         ],
         compiler_params=pltpu.CompilerParams(
-            collective_id=0, has_side_effects=True, vmem_limit_bytes=48 * 1024 * 1024
+            collective_id=0, has_side_effects=True, vmem_limit_bytes=57 * 1024 * 1024
         ),
         name="relay",
     )(order, blocks_of, inputs, cotangent, weights)
@@ -507,7 +526,7 @@
         out_specs=(*(vmem for _ in shapes), vmem),
         scratch_shapes=[dma((n + 1, 26)), dma((n + 1, 26)), *scratch],
         compiler_params=pltpu.CompilerParams(
-            collective_id=1, has_side_effects=True, vmem_limit_bytes=44 * 1024 * 1024
+            collective_id=1, has_side_effects=True, vmem_limit_bytes=32 * 1024 * 1024
         ),
         name="dp_part",
     )(turned, slopes, precond, squares)

time: 174 us -> 157 us (0.902)
  Pallas kernels: 169 us -> 155 us
  local copies, waits for them, and re-layouts: 3.32 us -> 0.01 us
    pallas_call x1, Pallas kernels: 67.6 us -> 53.1 us  [relay(): pl.pallas_call(relay_kernel, out_shape=(pltpu.VMEM((4, 4, 2, 64, n_micro...]
    unnamed x10 -> x4, local copies, waits for them, and re-layouts: 3.32 us -> 0.01 us
where the time goes in v4:
time: 157 us
  Pallas kernels  155 us (99%)
    pallas_call x1, Pallas kernels, dp_part(): pl.pallas_call(dp_kernel, out_shape=(*(pltpu.VMEM(shape, bf) for shape in...  95.6 us
    pallas_call x1, Pallas kernels, relay(): pl.pallas_call(relay_kernel, out_shape=(pltpu.VMEM((4, 4, 2, 64, n_micro...  53.1 us
    pallas_call x1, Pallas kernels, restore(): pl.pallas_call(restore_kernel, out_shape=(jax.ShapeDtypeStruct((32, 64, w...  6.03 us

profile of v4, /device:TPU:0, one launch (start us, length us, event | category | flops | bytes accessed | tf_op | source)
XLA Modules:
  0.0 156.9 jit_solution(7064473108430280788)
XLA Ops:
  0.6 1.3 select_reduce_fusion.blocks_ref
  1.9 0.0 copy-start
  1.9 53.1 %relay.1 = (bf16[4,4,2,64,512]{4,3,2,1,0:T(8,128)(2,1)S(1)}, bf16[4,128,2048]{2,1,0:T(8,128)(2,1)S(1)}, bf16[4,2,2,2,64,128]{5,4,3,2,1,0:T(8,128)(2,1)S(1)}) custom-call(s32[4]{0:T(128)} %bitcast.5, s32[32]{0:T(128)} %select_reduce_fusion.blocks_ref, bf16[4,128,2048]{2,1,0:T(8,128)(2,1)} %inputs_ref.1, bf16[4,128,2048]{2,1,0:T(8,128)(2,1)} %cot_ref.1, ...), custom_call_target="tpu_custom_call" | custom-call | tf_op jit(solution)/shard_map/relay/pallas_call | solution.py:256
  55.1 0.0 copy-done
  55.1 0.0 copy-start.1
  55.1 95.6 %dp_part.1 = (bf16[2,4,4,64,256]{4,3,2,1,0:T(8,128)(2,1)S(1)}, bf16[2,4,4,64,256]{4,3,2,1,0:T(8,128)(2,1)S(1)}, bf16[4,4,2,64,256]{4,3,2,1,0:T(8,128)(2,1)S(1)},...) custom-call(bf16[4,4,2,64,512]{4,3,2,1,0:T(8,128)(2,1)S(1)} %get-tup, ...), custom_call_target="tpu_custom_call" | custom-call | tf_op jit(solution)/shard_map/dp_part/pallas_call | solution.py:522
  150.7 0.0 copy-done.1
  150.7 6.0 %restore.1 = (bf16[32,64,2048]{2,1,0:T(8,128)(2,1)}, f32[64,64]{1,0:T(8,128)}) custom-call(s32[32]{0:T(128)S(1)} %copy-done.1, bf16[2,4,4,64,256]{4,3,2,1,0:T(8,128)(2,1)S(1)} %get-tuple-element.19.refs_0_, bf16[2,4,4,64,256]{4,3,2,1,0:T(8,128)(2,1)S(1)} %get-tuple-element.20.refs_1_, bf16[4,4,2,64,256]{4,3,2,1,0:T(8,128)(2,1)S(1)} %get-tuple-element.21.refs_2_, ...), custom_call_target="tpu_custom_call" | custom-call | tf_op jit(solution)/shard_map/restore/pallas_call | solution.py:571
Async XLA Ops:
  1.9 53.2 %copy-start = (f32[1,1,64,64]{3,2,1,0:T(8,128)S(1)}, f32[1,1,64,64]{3,2,1,0:T(8,128)}, u32[]{:S(2)}) copy-start(f32[1,1,64,64]{3,2,1,0:T(8,128)} %param.9) | copy-start | bytes 49156
  55.1 95.6 %copy-start.1 = (s32[32]{0:T(128)S(1)}, s32[32]{0:T(128)}, u32[]{:S(2)}) copy-start(s32[32]{0:T(128)} %owner_ref.1) | copy-start | bytes 388

commit v5 on v4

--- a/solution.py
+++ b/solution.py
@@ -17,7 +17,7 @@
 
 def relay_kernel(
     order_ref,
-    blocks_ref,
+    owner_ref,
     inputs_ref,
     cot_ref,
     weight_ref,
@@ -34,6 +34,7 @@
     back,
     total,
     flipped,
+    blocks_ref,
     w_sem,
     in_sem,
     f_send,
@@ -50,6 +51,13 @@
     for dev in ((s + 1) % 4, (s + 3) % 4):
         pl.semaphore_signal(barrier, inc=1, device_id={"section": dev}, device_id_type=MESH)
 
+    def find(p, carry):
+        block = jnp.int32(0)
+        for b in range(32):
+            block = jnp.where(owner_ref[b] == p, jnp.int32(b), block)
+        blocks_ref[p] = block
+        return carry
+
     def tile(t):
         return slice(t * TILE, (t + 1) * TILE)
 
@@ -71,6 +79,7 @@
         cot_copy.start()
 
     g_part[...] = jnp.zeros(g_part.shape, g_part.dtype)
+    lax.fori_loop(0, 32, find, 0)
     pl.semaphore_wait(barrier, 2)
 
     @pl.when(s == 0)
@@ -114,7 +123,7 @@
     def forward(k):
         @pl.when(s == 0)
         def _():
-            held[k] = feed[order_ref[k]]
+            held[k] = feed[order_ref[k // 2] * 2 + k % 2]
 
         for j in range(n_tiles):
 
@@ -173,12 +182,12 @@
                     back[k, :, tile(t)] = (g + value).astype(jnp.bfloat16)
                     backward_copy(k, t).start()
 
-    def turn(k):
+    def turn(m):
         for part in range(8):
-            block = held[k, :, part * 256 : (part + 1) * 256].T
-            flipped[part * 4 : (part + 1) * 4] = block.reshape(4, 64, rows)
-
-        lanes = pl.ds(pl.multiple_of(k * rows, rows), rows)
+            pair = held[pl.ds(m * 2, 2), :, part * 256 : (part + 1) * 256]
+            flipped[part * 4 : (part + 1) * 4] = pair.reshape(2 * rows, 256).T.reshape(4, 64, 2 * rows)
+
+        lanes = pl.ds(pl.multiple_of(m * 2 * rows, 2 * rows), 2 * rows)
 
         def move(p, carry):
             turned_ref[p // 8, (p // 2) % 4, p % 2, :, lanes] = flipped[blocks_ref[p]]
@@ -205,15 +214,15 @@
         def _():
             turn_weight()
 
-        b = k - jnp.where(s < 2, last, last - s)
+        b = k - jnp.where(s < 2, n_micro - 1, (last - s) * 2)
 
         @pl.when((b >= 0) & (b < n_micro))
         def _():
             backward(b)
 
-        @pl.when(k < n_micro)
-        def _():
-            turn(k)
+        @pl.when((k < n_micro) & (k % 2 == 1))
+        def _():
+            turn(k // 2)
 
         @pl.when(k == n_micro - 1)
         def _():
@@ -227,7 +236,7 @@
             w_copy(t).wait()
         turn_weight()
 
-    lax.fori_loop(0, n_micro + last, step, 0)
+    lax.fori_loop(0, 2 * n_micro - 1, step, 0)
 
     def drain(k, carry):
         @pl.when(s < last)
@@ -245,8 +254,9 @@
     lax.fori_loop(0, n_micro, drain, 0)
 
 
-def relay(inputs, cotangent, weights, order, blocks_of):
-    n_micro, rows, width = inputs.shape
+def relay(inputs, cotangent, weights, order, owner):
+    n_micro, rows, width = inputs.shape[0] * 2, inputs.shape[1] // 2, inputs.shape[2]
+    inputs, cotangent = (array.reshape(n_micro, rows, width) for array in (inputs, cotangent))
     n_tiles = width // TILE
     bf = jnp.bfloat16
     hbm, vmem = pl.BlockSpec(memory_space=pl.ANY), pl.BlockSpec(memory_space=pltpu.VMEM)
@@ -272,7 +282,8 @@
             block,
             block,
             pltpu.VMEM((rows, width), jnp.float32),
-            pltpu.VMEM((32, 64, rows), bf),
+            pltpu.VMEM((32, 64, 2 * rows), bf),
+            pltpu.SMEM((32,), jnp.int32),
             dma((n_tiles,)),
             dma(()),
             dma((n_micro, n_tiles)),
@@ -284,7 +295,7 @@
             collective_id=0, has_side_effects=True, vmem_limit_bytes=57 * 1024 * 1024
         ),
         name="relay",
-    )(order, blocks_of, inputs, cotangent, weights)
+    )(order, owner, inputs, cotangent, weights)
 
 
 SIZES = {"x": 4, "z": 4, "y": 2}
@@ -539,28 +550,18 @@
     gram_copy = pltpu.make_async_copy(gram_ref, gram_out, gram_sem)
     gram_copy.start()
 
-    def puts(b):
+    def first(b, carry):
         o = owner_ref[b]
         at = {"z": o // 8, "x": (o // 2) % 4, "y": o % 2}
-        copies, offset = [], 0
+        offset = 0
         for c, (dims, wide) in enumerate(CHUNKS):
             src = sources[c].at[tuple(at[d] for d in dims)]
-            copies.append(pltpu.make_async_copy(src, dst_ref.at[b, :, pl.ds(offset, wide)], sem.at[b, c]))
+            pltpu.make_async_copy(src, dst_ref.at[b, :, pl.ds(offset, wide)], sem).start()
             offset += wide
-        return copies
-
-    def first(b, carry):
-        for copy in puts(b):
-            copy.start()
         return carry
 
-    def second(b, carry):
-        for copy in puts(b):
-            copy.wait()
-        return carry
-
-    lax.fori_loop(0, 32, first, 0)
-    lax.fori_loop(0, 32, second, 0)
+    lax.fori_loop(0, 32, first, 0, unroll=4)
+    pltpu.make_async_copy(dst_ref, dst_ref, sem).wait()
     gram_copy.wait()
 
 
@@ -577,7 +578,7 @@
         in_specs=[pl.BlockSpec(memory_space=pltpu.SMEM), *[pl.BlockSpec(memory_space=pltpu.VMEM)] * (n + 1)],
         out_specs=(hbm, hbm),
         scratch_shapes=[
-            pltpu.SemaphoreType.DMA((32, n)),
+            pltpu.SemaphoreType.DMA(()),
             pltpu.SemaphoreType.DMA(()),
         ],
         compiler_params=pltpu.CompilerParams(vmem_limit_bytes=16 * 1024 * 1024),
@@ -587,11 +588,7 @@
 
 def body(inputs, cotangent, weights, preconds, order, owner):
     width = inputs.shape[2]
-    n_group = owner.shape[0]
-    positions = jnp.arange(n_group, dtype=jnp.int32)
-    matches = (owner[None, :] == positions[:, None]).astype(jnp.int32)
-    blocks_of = jnp.sum(matches * positions[None, :], axis=1)
-    turned, slopes, squares = relay(inputs, cotangent, weights, order[0], blocks_of)
+    turned, slopes, squares = relay(inputs, cotangent, weights, order[0], owner)
     gathered, gram = dp_part(turned, slopes, preconds[0, 0], squares)
     result, gram = restore(gathered, gram, owner)
     result = result.reshape(1, width, width)

time: 157 us -> 163 us (1.038)
  Pallas kernels: 155 us -> 162 us
    pallas_call x1, Pallas kernels: 53.1 us -> 65 us  [relay(): pl.pallas_call(relay_kernel, out_shape=(pltpu.VMEM((4, 4, 2, 64, n_micro...]
    pallas_call x1, Pallas kernels: 6.03 us -> 3.75 us  [restore(): pl.pallas_call(restore_kernel, out_shape=(jax.ShapeDtypeStruct((32, 64, w...]
    pallas_call x1, Pallas kernels: 95.6 us -> 93.5 us  [dp_part(): pl.pallas_call(dp_kernel, out_shape=(*(pltpu.VMEM(shape, bf) for shape in...]
where the time goes in v5:
time: 163 us
  Pallas kernels  162 us (99%)
    pallas_call x1, Pallas kernels, dp_part(): pl.pallas_call(dp_kernel, out_shape=(*(pltpu.VMEM(shape, bf) for shape in...  93.5 us
    pallas_call x1, Pallas kernels, relay(): pl.pallas_call(relay_kernel, out_shape=(pltpu.VMEM((4, 4, 2, 64, n_micro...  65 us
    pallas_call x1, Pallas kernels, restore(): pl.pallas_call(restore_kernel, out_shape=(jax.ShapeDtypeStruct((32, 64, w...  3.75 us

profile of v5, /device:TPU:0, one launch (start us, length us, event | category | flops | bytes accessed | tf_op | source)
XLA Modules:
  0.0 163.1 jit_solution(6334844351688499753)
XLA Ops:
  0.6 0.0 copy-start
  0.6 65.0 %relay.1 = (bf16[4,4,2,64,512]{4,3,2,1,0:T(8,128)(2,1)S(1)}, bf16[8,64,2048]{2,1,0:T(8,128)(2,1)S(1)}, bf16[4,2,2,2,64,128]{5,4,3,2,1,0:T(8,128)(2,1)S(1)}) custom-call(s32[4]{0:T(128)} %bitcast.9, s32[32]{0:T(128)} %owner_ref.3, bf16[8,64,2048]{2,1,0:T(8,128)(2,1)} %bitcast.7, bf16[8,64,2048]{2,1,0:T(8,128)(2,1)} %bitcast.8, bf16[1,2048,2048]{2,1,0:T(8,128)(2,1)} %weight_ref.1), custom_call_target="tpu_custom_call" | custom-call | tf_op jit(solution)/shard_map/relay/pallas_call | solution.py:266
  65.6 0.0 copy-done
  65.6 0.0 copy-start.1
  65.7 93.5 %dp_part.1 = (bf16[2,4,4,64,256]{4,3,2,1,0:T(8,128)(2,1)S(1)}, bf16[2,4,4,64,256]{4,3,2,1,0:T(8,128)(2,1)S(1)}, bf16[4,4,2,64,256]{4,3,2,1,0:T(8,128)(2,1)S(1)},...) custom-call(bf16[4,4,2,64,512]{4,3,2,1,0:T(8,128)(2,1)S(1)} %get-tup, ...), custom_call_target="tpu_custom_call" | custom-call | tf_op jit(solution)/shard_map/dp_part/pallas_call | solution.py:533
  159.1 0.0 copy-done.1
  159.2 3.8 %restore.1 = (bf16[32,64,2048]{2,1,0:T(8,128)(2,1)}, f32[64,64]{1,0:T(8,128)}) custom-call(s32[32]{0:T(128)S(1)} %copy-done.1, bf16[2,4,4,64,256]{4,3,2,1,0:T(8,128)(2,1)S(1)} %get-tuple-element.19.refs_0_, bf16[2,4,4,64,256]{4,3,2,1,0:T(8,128)(2,1)S(1)} %get-tuple-element.20.refs_1_, bf16[4,4,2,64,256]{4,3,2,1,0:T(8,128)(2,1)S(1)} %get-tuple-element.21.refs_2_, ...), custom_call_target="tpu_custom_call" | custom-call | tf_op jit(solution)/shard_map/restore/pallas_call | solution.py:572
Async XLA Ops:
  0.6 65.0 %copy-start = (f32[1,1,64,64]{3,2,1,0:T(8,128)S(1)}, f32[1,1,64,64]{3,2,1,0:T(8,128)}, u32[]{:S(2)}) copy-start(f32[1,1,64,64]{3,2,1,0:T(8,128)} %param.9) | copy-start | bytes 49156
  65.6 93.5 %copy-start.1 = (s32[32]{0:T(128)S(1)}, s32[32]{0:T(128)}, u32[]{:S(2)}) copy-start(s32[32]{0:T(128)} %owner_ref.3) | copy-start | bytes 388

commit v6 on v5

--- a/solution.py
+++ b/solution.py
@@ -123,7 +123,7 @@
     def forward(k):
         @pl.when(s == 0)
         def _():
-            held[k] = feed[order_ref[k // 2] * 2 + k % 2]
+            held[k] = feed[order_ref[k]]
 
         for j in range(n_tiles):
 
@@ -182,12 +182,12 @@
                     back[k, :, tile(t)] = (g + value).astype(jnp.bfloat16)
                     backward_copy(k, t).start()
 
-    def turn(m):
+    def turn(k):
         for part in range(8):
-            pair = held[pl.ds(m * 2, 2), :, part * 256 : (part + 1) * 256]
-            flipped[part * 4 : (part + 1) * 4] = pair.reshape(2 * rows, 256).T.reshape(4, 64, 2 * rows)
-
-        lanes = pl.ds(pl.multiple_of(m * 2 * rows, 2 * rows), 2 * rows)
+            block = held[k, :, part * 256 : (part + 1) * 256].T
+            flipped[part * 4 : (part + 1) * 4] = block.reshape(4, 64, rows)
+
+        lanes = pl.ds(pl.multiple_of(k * rows, rows), rows)
 
         def move(p, carry):
             turned_ref[p // 8, (p // 2) % 4, p % 2, :, lanes] = flipped[blocks_ref[p]]
@@ -214,15 +214,15 @@
         def _():
             turn_weight()
 
-        b = k - jnp.where(s < 2, n_micro - 1, (last - s) * 2)
+        b = k - jnp.where(s < 2, last, last - s)
 
         @pl.when((b >= 0) & (b < n_micro))
         def _():
             backward(b)
 
-        @pl.when((k < n_micro) & (k % 2 == 1))
-        def _():
-            turn(k // 2)
+        @pl.when(k < n_micro)
+        def _():
+            turn(k)
 
         @pl.when(k == n_micro - 1)
         def _():
@@ -236,7 +236,7 @@
             w_copy(t).wait()
         turn_weight()
 
-    lax.fori_loop(0, 2 * n_micro - 1, step, 0)
+    lax.fori_loop(0, n_micro + last, step, 0)
 
     def drain(k, carry):
         @pl.when(s < last)
@@ -255,8 +255,7 @@
 
 
 def relay(inputs, cotangent, weights, order, owner):
-    n_micro, rows, width = inputs.shape[0] * 2, inputs.shape[1] // 2, inputs.shape[2]
-    inputs, cotangent = (array.reshape(n_micro, rows, width) for array in (inputs, cotangent))
+    n_micro, rows, width = inputs.shape
     n_tiles = width // TILE
     bf = jnp.bfloat16
     hbm, vmem = pl.BlockSpec(memory_space=pl.ANY), pl.BlockSpec(memory_space=pltpu.VMEM)
@@ -282,7 +281,7 @@
             block,
             block,
             pltpu.VMEM((rows, width), jnp.float32),
-            pltpu.VMEM((32, 64, 2 * rows), bf),
+            pltpu.VMEM((32, 64, rows), bf),
             pltpu.SMEM((32,), jnp.int32),
             dma((n_tiles,)),
             dma(()),

time: 163 us -> 153 us (0.939)
  Pallas kernels: 162 us -> 152 us
    pallas_call x1, Pallas kernels: 65 us -> 53.1 us  [relay(): pl.pallas_call(relay_kernel, out_shape=(pltpu.VMEM((4, 4, 2, 64, n_micro...]
    pallas_call x1, Pallas kernels: 93.5 us -> 95.6 us  [dp_part(): pl.pallas_call(dp_kernel, out_shape=(*(pltpu.VMEM(shape, bf) for shape in...]
where the time goes in v6:
time: 153 us
  Pallas kernels  152 us (99%)
    pallas_call x1, Pallas kernels, dp_part(): pl.pallas_call(dp_kernel, out_shape=(*(pltpu.VMEM(shape, bf) for shape in...  95.6 us
    pallas_call x1, Pallas kernels, relay(): pl.pallas_call(relay_kernel, out_shape=(pltpu.VMEM((4, 4, 2, 64, n_micro...  53.1 us
    pallas_call x1, Pallas kernels, restore(): pl.pallas_call(restore_kernel, out_shape=(jax.ShapeDtypeStruct((32, 64, w...  3.75 us

profile of v6, /device:TPU:0, one launch (start us, length us, event | category | flops | bytes accessed | tf_op | source)
XLA Modules:
  0.0 153.3 jit_solution(16740969314109784380)
XLA Ops:
  0.6 0.0 copy-start
  0.6 53.1 %relay.1 = (bf16[4,4,2,64,512]{4,3,2,1,0:T(8,128)(2,1)S(1)}, bf16[4,128,2048]{2,1,0:T(8,128)(2,1)S(1)}, bf16[4,2,2,2,64,128]{5,4,3,2,1,0:T(8,128)(2,1)S(1)}) custom-call(s32[4]{0:T(128)} %bitcast.5, s32[32]{0:T(128)} %owner_ref.3, bf16[4,128,2048]{2,1,0:T(8,128)(2,1)} %inputs_ref.1, bf16[4,128,2048]{2,1,0:T(8,128)(2,1)} %cot_ref.1, ...), custom_call_target="tpu_custom_call" | custom-call | tf_op jit(solution)/shard_map/relay/pallas_call | solution.py:265
  53.7 0.0 copy-done
  53.7 0.0 copy-start.1
  53.8 95.6 %dp_part.1 = (bf16[2,4,4,64,256]{4,3,2,1,0:T(8,128)(2,1)S(1)}, bf16[2,4,4,64,256]{4,3,2,1,0:T(8,128)(2,1)S(1)}, bf16[4,4,2,64,256]{4,3,2,1,0:T(8,128)(2,1)S(1)},...) custom-call(bf16[4,4,2,64,512]{4,3,2,1,0:T(8,128)(2,1)S(1)} %get-tup, ...), custom_call_target="tpu_custom_call" | custom-call | tf_op jit(solution)/shard_map/dp_part/pallas_call | solution.py:532
  149.3 0.0 copy-done.1
  149.4 3.8 %restore.1 = (bf16[32,64,2048]{2,1,0:T(8,128)(2,1)}, f32[64,64]{1,0:T(8,128)}) custom-call(s32[32]{0:T(128)S(1)} %copy-done.1, bf16[2,4,4,64,256]{4,3,2,1,0:T(8,128)(2,1)S(1)} %get-tuple-element.19.refs_0_, bf16[2,4,4,64,256]{4,3,2,1,0:T(8,128)(2,1)S(1)} %get-tuple-element.20.refs_1_, bf16[4,4,2,64,256]{4,3,2,1,0:T(8,128)(2,1)S(1)} %get-tuple-element.21.refs_2_, ...), custom_call_target="tpu_custom_call" | custom-call | tf_op jit(solution)/shard_map/restore/pallas_call | solution.py:571
Async XLA Ops:
  0.6 53.1 %copy-start = (f32[1,1,64,64]{3,2,1,0:T(8,128)S(1)}, f32[1,1,64,64]{3,2,1,0:T(8,128)}, u32[]{:S(2)}) copy-start(f32[1,1,64,64]{3,2,1,0:T(8,128)} %param.9) | copy-start | bytes 49156
  53.7 95.6 %copy-start.1 = (s32[32]{0:T(128)S(1)}, s32[32]{0:T(128)}, u32[]{:S(2)}) copy-start(s32[32]{0:T(128)} %owner_ref.3) | copy-start | bytes 388

commit v7 on v6

--- a/solution.py
+++ b/solution.py
@@ -12,7 +12,7 @@
 cubic = 0.044715
 
 
-TILE = 512
+TILE = 1024
 
 
 def relay_kernel(

time: 153 us -> 153 us (level)
    pallas_call x1, Pallas kernels: 53.1 us -> 51.5 us  [relay(): pl.pallas_call(relay_kernel, out_shape=(pltpu.VMEM((4, 4, 2, 64, n_micro...]
where the time goes in v7:
time: 153 us
  Pallas kernels  152 us (99%)
    pallas_call x1, Pallas kernels, dp_part(): pl.pallas_call(dp_kernel, out_shape=(*(pltpu.VMEM(shape, bf) for shape in...  96.4 us
    pallas_call x1, Pallas kernels, relay(): pl.pallas_call(relay_kernel, out_shape=(pltpu.VMEM((4, 4, 2, 64, n_micro...  51.5 us
    pallas_call x1, Pallas kernels, restore(): pl.pallas_call(restore_kernel, out_shape=(jax.ShapeDtypeStruct((32, 64, w...  3.75 us

profile of v7, /device:TPU:0, one launch (start us, length us, event | category | flops | bytes accessed | tf_op | source)
XLA Modules:
  0.0 152.6 jit_solution(5635484968331168413)
XLA Ops:
  0.6 0.0 copy-start
  0.6 51.5 %relay.1 = (bf16[4,4,2,64,512]{4,3,2,1,0:T(8,128)(2,1)S(1)}, bf16[4,128,2048]{2,1,0:T(8,128)(2,1)S(1)}, bf16[4,2,2,2,64,128]{5,4,3,2,1,0:T(8,128)(2,1)S(1)}) custom-call(s32[4]{0:T(128)} %bitcast.5, s32[32]{0:T(128)} %owner_ref.3, bf16[4,128,2048]{2,1,0:T(8,128)(2,1)} %inputs_ref.1, bf16[4,128,2048]{2,1,0:T(8,128)(2,1)} %cot_ref.1, ...), custom_call_target="tpu_custom_call" | custom-call | tf_op jit(solution)/shard_map/relay/pallas_call | solution.py:265
  52.2 0.0 copy-done
  52.2 0.0 copy-start.1
  52.2 96.4 %dp_part.1 = (bf16[2,4,4,64,256]{4,3,2,1,0:T(8,128)(2,1)S(1)}, bf16[2,4,4,64,256]{4,3,2,1,0:T(8,128)(2,1)S(1)}, bf16[4,4,2,64,256]{4,3,2,1,0:T(8,128)(2,1)S(1)},...) custom-call(bf16[4,4,2,64,512]{4,3,2,1,0:T(8,128)(2,1)S(1)} %get-tup, ...), custom_call_target="tpu_custom_call" | custom-call | tf_op jit(solution)/shard_map/dp_part/pallas_call | solution.py:532
  148.6 0.0 copy-done.1
  148.6 3.8 %restore.1 = (bf16[32,64,2048]{2,1,0:T(8,128)(2,1)}, f32[64,64]{1,0:T(8,128)}) custom-call(s32[32]{0:T(128)S(1)} %copy-done.1, bf16[2,4,4,64,256]{4,3,2,1,0:T(8,128)(2,1)S(1)} %get-tuple-element.19.refs_0_, bf16[2,4,4,64,256]{4,3,2,1,0:T(8,128)(2,1)S(1)} %get-tuple-element.20.refs_1_, bf16[4,4,2,64,256]{4,3,2,1,0:T(8,128)(2,1)S(1)} %get-tuple-element.21.refs_2_, ...), custom_call_target="tpu_custom_call" | custom-call | tf_op jit(solution)/shard_map/restore/pallas_call | solution.py:571
Async XLA Ops:
  0.6 51.6 %copy-start = (f32[1,1,64,64]{3,2,1,0:T(8,128)S(1)}, f32[1,1,64,64]{3,2,1,0:T(8,128)}, u32[]{:S(2)}) copy-start(f32[1,1,64,64]{3,2,1,0:T(8,128)} %param.9) | copy-start | bytes 49156
  52.2 96.4 %copy-start.1 = (s32[32]{0:T(128)S(1)}, s32[32]{0:T(128)}, u32[]{:S(2)}) copy-start(s32[32]{0:T(128)} %owner_ref.3) | copy-start | bytes 388
